TPU v7x, 128 devices: a whole 4x4x4 slice. The times are simulated.
128 devices in a mesh: dp: 8 (over x, core), mp: 16 (over z, y).
Axes of the slice: x: 4, y: 4, z: 4, core: 2. Of those that a mesh axis runs over, the one named last changes fastest.
Arguments:
- canvas: bfloat16 [16, 16, 16, 1408], P('dp'), may hold values from -6 to 6
- target: bfloat16 [16, 16, 16, 1408], P('dp'), may hold values from -6 to 6
- kernel: float32 [49, 1408], replicated, may hold values from -0.875 to 0.875
- kernel_bias: float32 [1408], replicated, may hold values from -3 to 3
- norm_gain: float32 [1408], replicated, may hold values from 0.5 to 1.5
- norm_bias: float32 [1408], replicated, may hold values from -2 to 2
- in_weight: bfloat16 [5632, 1408], P('mp'), may hold values from -0.15625 to 0.15625
- in_bias: float32 [5632], P('mp'), may hold values from -3 to 3
- out_weight: bfloat16 [5632, 1408], P('mp'), may hold values from -0.078125 to 0.078125
- out_bias: float32 [1408], replicated, may hold values from -3 to 3
- probe_vector: float32 [49, 1408], P(None, 'mp'), may hold values from -6 to 6
- shapes: int32 [16, 2], P('dp'), may hold values from 2 to 16, as said below
- send_slots: int32 [16, 16, 16], P('dp'), may hold values from -1 to 447, as said below
Outputs:
- krylov_vector: float32 [49, 1408], P(None, 'mp')
- first_rayleigh: float32 [1], replicated
- lanczos_terms: float32 [3], replicated
Inputs may be any that keep to these rules, and one draw needn't show every extreme that they name: `shapes`: one of an image's two sides equals 16. `send_slots`: A cell's entry is -1 exactly where it lies outside its image; otherwise it is d * 56 + k: the cell goes to slot k of the owner with dp index d. No two cells of one dp index share an entry, so none sends more than 56 cells to one owner; every owner receives exactly 256 cells over all dp indices; some dp index sends 56 cells to every owner.
All inputs are finite; a program needn't handle non-finite values.
Results may differ from a plain program's by a relative error of at most 0.025.
Values may be sent and summed in bfloat16 or wider, within the bound.
A program may use at most 128 MiB of HBM per device.

v0:
```python
import jax
import jax.numpy as jnp
from jax import lax
from jax.sharding import PartitionSpec as P

C = 1408
KS = 7
SIDE = 16
MOST_SRC = 448
OWN = 256


layer_eps = 1e-06
vector_eps = 1e-06
half_root = 0.7071067811865476
density_scale = 0.3989422804014327


def phi_density(values):
    return density_scale * jnp.exp(-0.5 * values * values)


def gelu_value(values):
    return 0.5 * values * (1.0 + jax.scipy.special.erf(values * half_root))


def gelu_slope(values):
    return 0.5 * (1.0 + jax.scipy.special.erf(values * half_root)) + values * phi_density(values)


def gelu_bend(values):
    return phi_density(values) * (2.0 - values * values)


def inside_mask(shapes):
    cell_axis = jnp.arange(SIDE, dtype=jnp.int32)
    tall = cell_axis[None, :, None] < shapes[:, 0][:, None, None]
    wide = cell_axis[None, None, :] < shapes[:, 1][:, None, None]
    return (tall & wide).astype(jnp.float32)


def depthwise(canvas_values, tap_weights):
    margin_cells = KS // 2
    padded = jnp.pad(
        canvas_values, ((0, 0), (margin_cells, margin_cells), (margin_cells, margin_cells), (0, 0))
    )
    running = jnp.zeros(canvas_values.shape, jnp.float32)
    for tap_row in range(KS):
        for tap_col in range(KS):
            running = (
                running
                + padded[:, tap_row : tap_row + SIDE, tap_col : tap_col + SIDE, :]
                * tap_weights[tap_row * KS + tap_col]
            )
    return running


def correlate(masked, grads):
    margin_cells = KS // 2
    padded = jnp.pad(
        masked, ((0, 0), (margin_cells, margin_cells), (margin_cells, margin_cells), (0, 0))
    )
    pieces = []
    for tap_row in range(KS):
        for tap_col in range(KS):
            window = padded[:, tap_row : tap_row + SIDE, tap_col : tap_col + SIDE, :]
            pieces.append(
                jnp.einsum("npqc,npqc->c", window, grads, preferred_element_type=jnp.float32)
            )
    return jnp.stack(pieces, 0)


def normalize(rows):
    values = rows.astype(jnp.float32)
    row_mean = jnp.mean(values, 1, keepdims=True)
    centered = values - row_mean
    deviation = jnp.sqrt(jnp.mean(centered * centered, 1, keepdims=True) + layer_eps)
    return (centered / deviation, deviation)


def model_sum(partial_value):
    return lax.psum(partial_value.astype(jnp.bfloat16), "mp").astype(jnp.float32)


def input_share(partial_value):
    return lax.psum_scatter(
        partial_value.astype(jnp.bfloat16), "mp", scatter_dimension=1, tiled=True
    ).astype(jnp.float32)


def row_stats(first_sum, second_sum):
    return lax.psum((first_sum, second_sum), "mp")


def inner_model(first_vec, second_vec):
    return lax.psum(jnp.sum(first_vec * second_vec), "mp")


def alpha_of(product, direction):
    return inner_model(product, direction)


def per_device(
    canvas,
    target,
    kernel,
    kernel_bias,
    norm_gain,
    norm_bias,
    in_weight,
    in_bias,
    out_weight,
    out_bias,
    probe_vector,
    shapes,
    send_slots,
):
    sources = lax.axis_size("dp")
    models = lax.axis_size("mp")
    model_index = lax.axis_index("mp")
    images = canvas.shape[0]
    cell_count = images * SIDE * SIDE
    shard_width = C // models
    capacity = MOST_SRC // sources
    slot_count = sources * capacity
    tokens = OWN * sources
    channel_start = model_index * shard_width
    inside = inside_mask(shapes)
    masked = canvas * inside[..., None].astype(jnp.bfloat16)
    masked_part = lax.dynamic_slice_in_dim(masked, channel_start, shard_width, 3)
    flat_slots = send_slots.reshape(cell_count)
    slot_hits = flat_slots[None, :] == jnp.arange(slot_count, dtype=jnp.int32)[:, None]
    source_cell = jnp.sum(
        jnp.where(slot_hits, jnp.arange(cell_count, dtype=jnp.int32)[None, :], 0), axis=1
    )
    slot_flags = jnp.any(slot_hits, axis=1).astype(jnp.bfloat16).reshape(sources, capacity)

    def pack_slots(values):
        return jnp.take(values, source_cell, axis=0).reshape(sources, capacity, values.shape[1])

    conv_source = masked.astype(jnp.float32)
    conved = (depthwise(conv_source, kernel) + kernel_bias).astype(jnp.bfloat16)
    diff = (target.astype(jnp.float32) - canvas.astype(jnp.float32)).astype(jnp.bfloat16)
    payload = jnp.stack([conved.reshape(cell_count, C), diff.reshape(cell_count, C)], 1).reshape(
        cell_count, 2 * C
    )
    arrived_rows, arrived_flags = (
        lax.all_to_all(pack_slots(payload), "dp", split_axis=0, concat_axis=0, tiled=True),
        lax.all_to_all(slot_flags, "dp", split_axis=0, concat_axis=0, tiled=True),
    )
    gather_live_slots = arrived_flags.reshape(slot_count) > 0.5
    live_count = gather_live_slots.astype(jnp.int32)
    gather_position = jnp.cumsum(live_count) - live_count
    row_marks = gather_live_slots[None, :] & (
        gather_position[None, :] == jnp.arange(OWN, dtype=jnp.int32)[:, None]
    )
    gather_slot_of_row = jnp.sum(
        jnp.where(row_marks, jnp.arange(slot_count, dtype=jnp.int32)[None, :], 0), axis=1
    )
    owned_rows = jnp.take(
        arrived_rows.reshape(slot_count, 2 * C), gather_slot_of_row, axis=0
    ).reshape(OWN, 2, C)
    conv_rows = owned_rows[:, 0]
    diff_rows = owned_rows[:, 1]
    normed, deviation = normalize(conv_rows)
    features = (normed * norm_gain + norm_bias).astype(jnp.bfloat16)
    pre_act = (
        jnp.einsum("tc,hc->th", features, in_weight, preferred_element_type=jnp.float32) + in_bias
    )
    activation = gelu_value(pre_act).astype(jnp.bfloat16)
    outputs = (
        model_sum(jnp.dot(activation, out_weight, preferred_element_type=jnp.float32)) + out_bias
    )
    residue = (outputs - diff_rows.astype(jnp.float32)).astype(jnp.bfloat16)
    back_act = jnp.einsum("tc,hc->th", residue, out_weight, preferred_element_type=jnp.float32)
    slope = gelu_slope(pre_act)
    curvature = back_act * gelu_bend(pre_act)
    back_pre = (back_act * slope).astype(jnp.bfloat16)
    back_feat = input_share(jnp.dot(back_pre, in_weight, preferred_element_type=jnp.float32))
    gain_part = lax.dynamic_slice_in_dim(norm_gain, channel_start, shard_width, 0)
    normed_part = lax.dynamic_slice_in_dim(normed, channel_start, shard_width, 1)
    grad_scaled = back_feat * gain_part
    grad_total, grad_cross = row_stats(
        jnp.sum(grad_scaled, 1), jnp.sum(grad_scaled * normed_part, 1)
    )
    grad_mean = grad_total[:, None] / C
    grad_corr = grad_cross[:, None] / C
    back_conv = (grad_scaled - grad_mean - normed_part * grad_corr) / deviation
    safe_slots = jnp.maximum(flat_slots, 0)

    def hessian(direction):
        full_direction = lax.all_gather(direction, "mp", axis=1, tiled=True)
        tangent = depthwise(conv_source, full_direction).astype(jnp.bfloat16).reshape(cell_count, C)
        arrived_tan = lax.all_to_all(
            pack_slots(tangent), "dp", split_axis=0, concat_axis=0, tiled=True
        )
        tan_rows = jnp.take(arrived_tan.reshape(slot_count, C), gather_slot_of_row, axis=0)
        tangent_vals = tan_rows.astype(jnp.float32)
        lift = jnp.mean(normed * tangent_vals, 1, keepdims=True)
        tan_hat = (
            tangent_vals - jnp.mean(tangent_vals, 1, keepdims=True) - normed * lift
        ) / deviation
        rate = lift / deviation
        tan_feat = (tan_hat * norm_gain).astype(jnp.bfloat16)
        tan_pre = jnp.einsum("tc,hc->th", tan_feat, in_weight, preferred_element_type=jnp.float32)
        tan_act = (slope * tan_pre).astype(jnp.bfloat16)
        tan_out = model_sum(
            jnp.dot(tan_act, out_weight, preferred_element_type=jnp.float32)
        ).astype(jnp.bfloat16)
        tan_back_act = jnp.einsum(
            "tc,hc->th", tan_out, out_weight, preferred_element_type=jnp.float32
        )
        tan_back_pre = (tan_back_act * slope + curvature * tan_pre).astype(jnp.bfloat16)
        tan_scaled = (
            input_share(jnp.dot(tan_back_pre, in_weight, preferred_element_type=jnp.float32))
            * gain_part
        )
        tan_hat_part = lax.dynamic_slice_in_dim(tan_hat, channel_start, shard_width, 1)
        tan_total, tan_cross = row_stats(
            jnp.sum(tan_scaled, 1),
            jnp.sum(tan_scaled * normed_part + grad_scaled * tan_hat_part, 1),
        )
        tan_mean = tan_total[:, None] / C
        tan_corr = tan_cross[:, None] / C
        tan_back = (
            (tan_scaled - tan_mean - tan_hat_part * grad_corr - normed_part * tan_corr) / deviation
            - back_conv * rate
        ).astype(jnp.bfloat16)
        at_slots = jnp.take(tan_back, gather_position, axis=0)
        at_slots = jnp.where(gather_live_slots[:, None], at_slots, jnp.zeros_like(at_slots))
        returned = lax.all_to_all(
            at_slots.reshape(sources, capacity, shard_width),
            "dp",
            split_axis=0,
            concat_axis=0,
            tiled=True,
        )
        cell_values = jnp.take(returned.reshape(slot_count, shard_width), safe_slots, axis=0)
        cell_values = jnp.where(flat_slots[:, None] >= 0, cell_values, jnp.zeros_like(cell_values))
        local_term = correlate(
            masked_part, cell_values.reshape(images, SIDE, SIDE, shard_width)
        ) * (1.0 / tokens)
        return (lax.psum(local_term, "dp"), local_term)

    probe_norm = jnp.sqrt(inner_model(probe_vector, probe_vector) + vector_eps)
    lanczos_one = probe_vector / probe_norm
    product_one, local_one = hessian(lanczos_one)
    alpha_one = alpha_of(product_one, lanczos_one)
    remainder_one = product_one - alpha_one * lanczos_one
    beta_one = jnp.sqrt(inner_model(remainder_one, remainder_one) + vector_eps)
    lanczos_two = remainder_one / beta_one
    product_two, local_two = hessian(lanczos_two)
    alpha_two = alpha_of(product_two, lanczos_two)
    remainder_two = product_two - alpha_two * lanczos_two - beta_one * lanczos_one
    beta_two = jnp.sqrt(inner_model(remainder_two, remainder_two) + vector_eps)
    return (
        remainder_two / beta_two,
        jnp.stack([alpha_one]),
        jnp.stack([alpha_two, beta_one, beta_two]),
    )


def solution(mesh):
    placed = (
        P("dp", None, None, None),
        P("dp", None, None, None),
        P(),
        P(),
        P(),
        P(),
        P("mp", None),
        P("mp"),
        P("mp", None),
        P(),
        P(None, "mp"),
        P("dp", None),
        P("dp", None, None),
    )
    return jax.shard_map(
        per_device, mesh=mesh, in_specs=placed, out_specs=(P(None, "mp"), P(), P()), check_vma=False
    )
```

profile of v0, /device:TPU:0, one launch (start us, length us, event | category | flops | bytes accessed | tf_op | source)
XLA Modules:
  0.0 1089.0 jit_solution(18031086385054804951)
XLA Ops:
  9.0 4.4 all-to-all-start
  13.4 1.9 slice_reduce_fusion.146
  15.3 1.8 slice_reduce_fusion.145
  17.3 1.4 multiply_reduce_fusion.5
  20.0 42.6 %psum.112 = f32[]{:T(128)} all-reduce(f32[]{:T(128)} %multiply_reduce_fusion.5), channel_id=1, replica_groups=mesh['dp'=8,'mp'=16] {'mp'}, use_global_device_ids=true, to_apply=%region_8.9 | all-reduce | flops 1 | bytes 8 | tf_op jit(solution)/shard_map/psum | solution.py:96
  64.0 21.0 %all-gather = f32[16,88,49]{1,2,0:T(8,128)S(1)} all-gather(f32[1,88,49]{1,2,0:T(8,128)S(1)} %fusion.195), channel_id=1, replica_groups=mesh['dp'=8,'mp'=16] {'mp'}, dimensions={0}, use_global_device_ids=true | all-gather | bytes 293216 | tf_op jit(solution)/shard_map/all_gather | solution.py:192
  87.9 19.6 %add_convert_fusion.2 = bf16[2,16,16,1408]{3,2,1,0:T(8,128)(2,1)S(1)} fusion(bf16[2,16,16,1408]{3,2,1,0:T(8,128)(2,1)S(1)} %get-tuple-element.279, f32[2,16,16,1408]{3,2,1,0:T(8,128)S(1)} %get-tuple-element.278, f32[1408]{0:T(1024)S(1)} %copy-done.48, f32[1408]{0:T(1024)S(1)} %get-tuple-element.109, f32[1408]{0:T(1024)S(1)} %get-tuple-element.110, ...), kind=kLoop, calls=%fused_computation.160 | loop fusion | flops 72089600 | bytes 6048768 | tf_op jit(solution)/shard_map/convert_element_type | solution.py:142
  107.6 2.2 copy.51
  110.2 2.2 copy.52
  112.5 8.1 pad_maximum_fusion
  120.6 19.7 %add_convert_fusion.1 = bf16[2,16,16,1408]{3,2,1,0:T(8,128)(2,1)S(1)} fusion(bf16[2,16,16,1408]{3,2,1,0:T(8,128)(2,1)S(1)} %get-tuple-element.279, f32[2,16,16,1408]{3,2,1,0:T(8,128)S(1)} %get-tuple-element.278, f32[1408]{0:T(1024)S(1)} %get-tuple-element.112, f32[1408]{0:T(1024)S(1)} %get-tuple-element.113, f32[1408]{0:T(1024)S(1)} %get-tuple-element.114, ...), kind=kLoop, calls=%fused_computation.158 | loop fusion | flops 71368704 | bytes 6043136 | tf_op jit(solution)/shard_map/convert_element_type | solution.py:193
  140.3 2.9 gather_fusion.2
  143.2 2.6 broadcast_select_fusion.2
  145.9 3.8 copy.746
  149.7 4.8 all-to-all-start.2
  154.6 8.7 gather_fusion
  163.3 3.5 broadcast_select_fusion
  166.7 6.0 all-to-all-done.2
  173.9 3.6 all-to-all-start.1
  180.4 4.2 gather_fusion.3
  184.6 24.6 %all-to-all-done.1 = bf16[8,56,2816]{2,1,0:T(8,128)(2,1)S(1)} async-done(((bf16[8,56,2816]{2,1,0:T(8,128)(2,1)}), bf16[8,56,2816]{2,1,0:T(8,128)(2,1)S(1)}, u32[]{:S(2)}, u32[]{:S(2)}) %all-to-all-start.1) | async-done | bytes 2523168 | tf_op jit(solution)/shard_map/all_to_all | solution.py:148
  209.2 2.6 gather_fusion.1
  211.8 2.1 copy.53
  213.9 1.5 copy.54
  215.4 1.7 broadcast_select_fusion.1
  217.7 1.6 convert_reduce_fusion.1
  221.7 1.4 convolution_convert_fusion.4
  223.1 1.6 convolution_convert_fusion.5
  224.8 86.0 %all-reduce.14.cloned.1.call-done = (bf16[256,1408]{1,0:T(8,128)(2,1)}, bf16[256,1408]{1,0:T(8,128)(2,1)}) async-done(((bf16[256,1408]{1,0:T(8,128)(2,1)}, bf16[256,1408]{1,0:T(8,128)(2,1)}), (bf16[256,1408]{1,0:T(8,128)(2,1)}, bf16[256,1408]{1,0:T(8,128)(2,1)})) %all-reduce.14.cloned.1.call-update) | async-done | bytes 1441808 | tf_op jit(solution)/shard_map/psum | solution.py:82
  310.8 1.7 fusion.18
  313.2 1.6 convolution_convert_fusion.2
  315.0 3.7 convolution_convert_fusion.3
  319.9 67.5 %reduce-scatter.12.cloned.1.call-done = bf16[256,88]{0,1:T(8,128)(2,1)} async-done(((bf16[256,1408]{0,1:T(8,128)(2,1)}), bf16[256,88]{0,1:T(8,128)(2,1)}) %reduce-scatter.12.cloned.1.call-update) | async-done | bytes 45072
  388.4 74.6 %reduce-scatter.10.cloned.1.call-done = bf16[256,88]{0,1:T(8,128)(2,1)} async-done(((bf16[256,1408]{0,1:T(8,128)(2,1)}), bf16[256,88]{0,1:T(8,128)(2,1)}) %reduce-scatter.10.cloned.1.call-update) | async-done | bytes 45072
  463.9 1.4 multiply_reduce_fusion
  465.3 38.1 %all-reduce.7 = (f32[256]{0:T(256)S(1)}, f32[256]{0:T(256)S(1)}, f32[256]{0:T(256)S(1)}, f32[256]{0:T(256)S(1)}) all-reduce(f32[256]{0:T(256)S(1)} %get-tuple-element.261, f32[256]{0:T(256)S(1)} %get-tuple-element.8, f32[256]{0:T(256)S(1)} %get-tuple-element.6, f32[256]{0:T(256)S(1)} %get-tuple-element.258), channel_id=1, replica_groups=mesh['dp'=8,'mp'=16] {'mp'}, use_global_device_ids=true, to_apply=%region_22.25 | all-reduce | flops 1024 | bytes 8192 | tf_op jit(solution)/shard_map/psum | solution.py:92
  503.9 1.4 subtract_convert_fusion.2
  505.3 1.5 gather_fusion.4
  507.7 4.2 all-to-all-start.3
  512.0 5.9 all-to-all-done.3
  521.4 23.9 %psum.119 = f32[49,88]{1,0:T(8,128)S(1)} all-reduce(f32[49,88]{1,0:T(8,128)S(1)} %broadcast_multiply_fusion.2), channel_id=1, replica_groups=mesh['dp'=8,'mp'=16] {'dp'}, use_global_device_ids=true, to_apply=%region_23.28 | all-reduce | flops 4312 | bytes 34496 | tf_op jit(solution)/shard_map/psum | solution.py:243
  545.9 36.1 %psum.120 = f32[]{:T(128)} all-reduce(f32[]{:T(128)} %multiply_reduce_fusion.4), channel_id=1, replica_groups=mesh['dp'=8,'mp'=16] {'mp'}, use_global_device_ids=true, to_apply=%region_25.30 | all-reduce | flops 1 | bytes 8 | tf_op jit(solution)/shard_map/psum | solution.py:96
  583.2 38.1 %psum.121 = f32[]{:T(128)} all-reduce(f32[]{:T(128)} %multiply_reduce_fusion.3), channel_id=1, replica_groups=mesh['dp'=8,'mp'=16] {'mp'}, use_global_device_ids=true, to_apply=%region_27.32 | all-reduce | flops 1 | bytes 8 | tf_op jit(solution)/shard_map/psum | solution.py:96
  622.6 21.2 %all-gather.1 = f32[16,88,49]{1,2,0:T(8,128)S(1)} all-gather(f32[1,88,49]{1,2,0:T(8,128)S(1)} %fusion.194), channel_id=1, replica_groups=mesh['dp'=8,'mp'=16] {'mp'}, dimensions={0}, use_global_device_ids=true | all-gather | bytes 293216 | tf_op jit(solution)/shard_map/all_gather | solution.py:192
  644.9 80.7 %add_convert_fusion = bf16[2,16,16,1408]{3,2,1,0:T(8,128)(2,1)S(1)} fusion(bf16[2,16,16,1408]{3,2,1,0:T(8,128)(2,1)} %copy-done.3, f32[2,16,16,1408]{3,2,1,0:T(8,128)} %copy-done.1, f32[1408]{0:T(1024)S(1)} %get-tuple-element.14, f32[1408]{0:T(1024)S(1)} %get-tuple-element.15, f32[1408]{0:T(1024)S(1)} %get-tuple-element.16, f32[1408]{0:T(1024)S(1)} %get-tuple-element.17, ...), kind=kLoop, calls=%fused_computation.157 | loop fusion | flops 71368704 | bytes 6043136 | tf_op jit(solution)/shard_map/convert_element_type | solution.py:193
  725.6 3.0 gather_fusion.6
  728.6 1.5 broadcast_select_fusion.3
  730.1 20.7 %all_to_all.31 = bf16[8,56,1408]{2,1,0:T(8,128)(2,1)S(1)} all-to-all(bf16[8,56,1408]{2,1,0:T(8,128)(2,1)S(1)} %bitcast.832), channel_id=1, replica_groups=mesh['dp'=8,'mp'=16] {'dp'}, dimensions={0} | all-to-all | bytes 2523136 | tf_op jit(solution)/shard_map/all_to_all | solution.py:194
  750.8 2.4 gather_fusion.7
  753.2 1.9 convert_reduce_fusion
  755.6 1.8 fusion.8
  758.7 1.5 convolution_convert_fusion.1
  760.3 83.7 %all-reduce.12.cloned.1.call-done = bf16[256,1408]{1,0:T(8,128)(2,1)} async-done(((bf16[256,1408]{1,0:T(8,128)(2,1)}), bf16[256,1408]{1,0:T(8,128)(2,1)}) %all-reduce.12.cloned.1.call-update) | async-done | bytes 720912 | tf_op jit(solution)/shard_map/psum | solution.py:82
  844.0 3.9 convolution_convert_fusion
  848.0 72.4 %reduce-scatter.14.cloned.1.call-done = bf16[256,88]{0,1:T(8,128)(2,1)} async-done(((bf16[256,1408]{0,1:T(8,128)(2,1)}), bf16[256,88]{0,1:T(8,128)(2,1)}) %reduce-scatter.14.cloned.1.call-update) | async-done | bytes 45072
  922.6 38.1 %all-reduce.6 = (f32[256]{0:T(256)S(1)}, f32[256]{0:T(256)S(1)}) all-reduce(f32[256]{0:T(256)S(1)} %get-tuple-element.260, f32[256]{0:T(256)S(1)} %get-tuple-element.259), channel_id=1, replica_groups=mesh['dp'=8,'mp'=16] {'mp'}, use_global_device_ids=true, to_apply=%region_35.40 | all-reduce | flops 512 | bytes 4096 | tf_op jit(solution)/shard_map/psum | solution.py:92
  960.7 1.4 subtract_convert_fusion.1
  962.1 1.6 gather_fusion.8
  964.6 10.2 all_to_all.32
  974.8 1.3 gather_fusion.9
  978.3 23.9 %psum.125 = f32[49,88]{1,0:T(8,128)S(1)} all-reduce(f32[49,88]{1,0:T(8,128)S(1)} %broadcast_multiply_fusion.1), channel_id=1, replica_groups=mesh['dp'=8,'mp'=16] {'dp'}, use_global_device_ids=true, to_apply=%region_36.41 | all-reduce | flops 4312 | bytes 34496 | tf_op jit(solution)/shard_map/psum | solution.py:243
  1003.5 36.2 %psum.126 = f32[]{:T(128)} all-reduce(f32[]{:T(128)} %multiply_reduce_fusion.2), channel_id=1, replica_groups=mesh['dp'=8,'mp'=16] {'mp'}, use_global_device_ids=true, to_apply=%region_38.43 | all-reduce | flops 1 | bytes 8 | tf_op jit(solution)/shard_map/psum | solution.py:96
  1039.6 2.0 multiply_reduce_fusion.1
  1041.6 38.1 %psum.127 = f32[]{:T(128)} all-reduce(f32[]{:T(128)} %get-tuple-element.272), channel_id=1, replica_groups=mesh['dp'=8,'mp'=16] {'mp'}, use_global_device_ids=true, to_apply=%region_40.45 | all-reduce | flops 1 | bytes 8 | tf_op jit(solution)/shard_map/psum | solution.py:96
  (224 shorter events, 36.8 us)
Async XLA Ops:
  7.2 214.5 %copy-start = (bf16[352,1408]{1,0:T(8,128)(2,1)S(1)}, bf16[352,1408]{1,0:T(8,128)(2,1)}, u32[]{:S(2)}) copy-start(bf16[352,1408]{1,0:T(8,128)(2,1)} %param.29) | copy-start | bytes 2973700
  7.2 80.1 %copy-start.13 = (bf16[2,16,16,1408]{3,2,1,0:T(8,128)(2,1)S(1)}, bf16[2,16,16,1408]{3,2,1,0:T(8,128)(2,1)}, u32[]{:S(2)}) copy-start(bf16[2,16,16,1408]{3,2,1,0:T(8,128)(2,1)} %param.21) | copy-start | bytes 4325380
  8.1 55.9 %copy-start.24 = (s32[512]{0:T(512)}, s32[512]{0:T(512)S(1)}, u32[]{:S(2)}) copy-start(s32[512]{0:T(512)S(1)} %broadcast_in_dim_reshape.2) | copy-start | bytes 6148
  9.0 140.7 %all-to-all-start = ((bf16[8,1,56]{2,1,0:T(2,128)(2,1)}), bf16[8,1,56]{2,1,0:T(2,128)(2,1)}, u32[]{:S(2)}, u32[]{:S(2)}) async-start(bf16[8,1,56]{2,1,0:T(2,128)(2,1)} %reshape.856), calls=%async_computation | async-start | bytes 8192 | tf_op jit(solution)/shard_map/all_to_all | solution.py:149
  86.1 57.1 %copy-start.55 = (pred[448]{0:T(512)(128)(4,1)}, pred[448]{0:T(512)(128)(4,1)S(1)}, u32[]{:S(2)}) copy-start(pred[448]{0:T(512)(128)(4,1)S(1)} %compare_and_fusion.2) | copy-start | bytes 1348
  87.6 33.0 %copy-start.1 = (f32[2,16,16,1408]{3,2,1,0:T(8,128)}, f32[2,16,16,1408]{3,2,1,0:T(8,128)S(1)}, u32[]{:S(2)}) copy-start(f32[2,16,16,1408]{3,2,1,0:T(8,128)S(1)} %get-tuple-element.278) | copy-start | bytes 8650756
  87.6 33.0 %copy-start.3 = (bf16[2,16,16,1408]{3,2,1,0:T(8,128)(2,1)}, bf16[2,16,16,1408]{3,2,1,0:T(8,128)(2,1)S(1)}, u32[]{:S(2)}) copy-start(bf16[2,16,16,1408]{3,2,1,0:T(8,128)(2,1)S(1)} %get-tuple-element.279) | copy-start | bytes 4325380
  107.6 2.2 copy-start.18
  112.5 27.8 %copy-start.35 = (s32[1024]{0:T(1024)}, s32[1024]{0:T(1024)S(1)}, u32[]{:S(2)}) copy-start(s32[1024]{0:T(1024)S(1)} %pad_clamp_fusion.3) | copy-start | bytes 12292
  149.7 23.1 %all-to-all-start.2 = ((bf16[8,56,1408]{2,1,0:T(8,128)(2,1)}), bf16[8,56,1408]{2,1,0:T(8,128)(2,1)S(1)}, u32[]{:S(2)}, u32[]{:S(2)}) async-start(bf16[8,56,1408]{2,1,0:T(8,128)(2,1)} %bitcast.212), calls=%async_computation.2 | async-start | bytes 2523136 | tf_op jit(solution)/shard_map/all_to_all | solution.py:194
  172.8 1.1 copy-start.2
  173.9 35.3 %all-to-all-start.1 = ((bf16[8,56,2816]{2,1,0:T(8,128)(2,1)}), bf16[8,56,2816]{2,1,0:T(8,128)(2,1)S(1)}, u32[]{:S(2)}, u32[]{:S(2)}) async-start(bf16[8,56,2816]{2,1,0:T(8,128)(2,1)} %broadcast_select_fusion), calls=%async_computation.1 | async-start | bytes 5046272 | tf_op jit(solution)/shard_map/all_to_all | solution.py:148
  177.5 133.3 %all-reduce.14.cloned.1.call-start = ((), (), s32[]{:S(2)}) async-start(), calls=%async_computation.13 | async-start | bytes 2883584 | tf_op jit(solution)/shard_map/psum | solution.py:82
  178.3 6.2 copy-start.43
  180.3 4.3 copy-start.47
  180.3 39.5 %copy-start.41 = (pred[256]{0:T(512)(128)(4,1)}, pred[256]{0:T(512)(128)(4,1)S(1)}, u32[]{:S(2)}) copy-start(pred[256]{0:T(512)(128)(4,1)S(1)} %compare_and_fusion.3) | copy-start | bytes 772
  215.4 2.2 copy-start.8
  217.1 93.7 %copy-start.4 = (bf16[256,2,1408]{2,0,1:T(8,128)(2,1)}, bf16[256,2,1408]{2,0,1:T(8,128)(2,1)S(1)}, u32[]{:S(2)}) copy-start(bf16[256,2,1408]{2,0,1:T(8,128)(2,1)S(1)} %broadcast_select_fusion.1) | copy-start | bytes 4325380
  217.3 3.7 copy-start.29
  217.6 2.8 copy-start.39
  217.6 3.3 copy-start.26
  217.6 2.8 copy-start.5
  217.7 2.8 copy-start.31
  219.3 1.7 copy-start.57
  219.3 1.7 copy-start.59
  220.4 1.2 copy-start.6
  221.0 2.1 copy-start.15
  221.6 1.5 copy-start.9
  221.7 89.1 %copy-start.58 = (f32[1408]{0:T(1024)S(1)}, f32[1408]{0:T(1024)}, u32[]{:S(2)}) copy-start(f32[1408]{0:T(1024)} %param.30) | copy-start | bytes 16900
  224.7 162.8 %reduce-scatter.12.cloned.1.call-start = ((), (), s32[]{:S(2)}) async-start(), calls=%async_computation.11 | async-start | bytes 765952
  310.8 2.5 copy-start.10
  313.2 1.7 copy-start.11
  313.2 1.7 copy-start.16
  314.9 5.0 copy-start.25
  314.9 5.0 copy-start.34
  314.9 148.1 %reduce-scatter.10.cloned.1.call-start = ((), (), s32[]{:S(2)}) async-start(), calls=%async_computation.10 | async-start | bytes 765952
  315.0 189.0 %copy-start.27 = (f32[256]{0:T(256)S(1)}, f32[256]{0:T(256)}, u32[]{:S(2)}) copy-start(f32[256]{0:T(256)} %copy-done.26) | copy-start | bytes 3076
  315.0 189.0 %copy-start.56 = (f32[256]{0:T(256)S(1)}, f32[256]{0:T(256)}, u32[]{:S(2)}) copy-start(f32[256]{0:T(256)} %get-tuple-element.285) | copy-start | bytes 3076
  315.0 191.8 %copy-start.44 = (pred[448]{0:T(512)(128)(4,1)S(1)}, pred[448]{0:T(512)(128)(4,1)}, u32[]{:S(2)}) copy-start(pred[448]{0:T(512)(128)(4,1)} %copy-done.43) | copy-start | bytes 1348
  315.0 191.8 %copy-start.50 = (pred[448]{0:T(512)(128)(4,1)S(1)}, pred[448]{0:T(512)(128)(4,1)}, u32[]{:S(2)}) copy-start(pred[448]{0:T(512)(128)(4,1)} %get-tuple-element.276) | copy-start | bytes 1348
  318.7 226.6 %copy-start.19 = (f32[49,88]{1,0:T(8,128)S(1)}, f32[49,88]{1,0:T(8,128)}, u32[]{:S(2)}) copy-start(f32[49,88]{1,0:T(8,128)} %param.31) | copy-start | bytes 51748
  318.8 184.6 %copy-start.49 = (f32[88]{0:T(128)}, f32[88]{0:T(128)S(1)}, u32[]{:S(2)}) copy-start(f32[88]{0:T(128)S(1)} %dynamic_slice.16) | copy-start | bytes 1060
  319.9 324.0 %copy-start.51 = (pred[512]{0:T(512)(128)(4,1)}, pred[512]{0:T(512)(128)(4,1)S(1)}, u32[]{:S(2)}) copy-start(pred[512]{0:T(512)(128)(4,1)S(1)} %get-tuple-element.281) | copy-start | bytes 1540
  319.9 324.0 %copy-start.53 = (pred[512]{0:T(512)(128)(4,1)}, pred[512]{0:T(512)(128)(4,1)S(1)}, u32[]{:S(2)}) copy-start(pred[512]{0:T(512)(128)(4,1)S(1)} %get-tuple-element.282) | copy-start | bytes 1540
  319.9 199.3 %copy-start.36 = (s32[1024]{0:T(1024)}, s32[1024]{0:T(1024)S(1)}, u32[]{:S(2)}) copy-start(s32[1024]{0:T(1024)S(1)} %pad_clamp_fusion.1) | copy-start | bytes 12292
  388.4 119.3 %copy-start.14 = (bf16[256,88]{1,0:T(8,128)(2,1)}, bf16[256,88]{1,0:T(8,128)(2,1)S(1)}, u32[]{:S(2)}) copy-start(bf16[256,88]{1,0:T(8,128)(2,1)S(1)} %copy.57) | copy-start | bytes 135172
  503.4 140.6 %copy-start.45 = (f32[256]{0:T(256)}, f32[256]{0:T(256)S(1)}, u32[]{:S(2)}) copy-start(f32[256]{0:T(256)S(1)} %broadcast_multiply_fusion.7) | copy-start | bytes 3076
  507.7 10.2 all-to-all-start.3
  511.9 332.1 %all-reduce.12.cloned.1.call-start = ((), (), s32[]{:S(2)}) async-start(), calls=%async_computation.9 | async-start | bytes 1441792 | tf_op jit(solution)/shard_map/psum | solution.py:82
  512.0 7.2 copy-start.37
  545.2 77.4 %copy-start.21 = (f32[49,88]{1,0:T(8,128)}, f32[49,88]{1,0:T(8,128)S(1)}, u32[]{:S(2)}) copy-start(f32[49,88]{1,0:T(8,128)S(1)} %psum.119) | copy-start | bytes 51748
  750.8 2.4 copy-start.28
  750.8 2.4 copy-start.30
  750.8 2.4 copy-start.42
  750.8 4.3 copy-start.40
  753.2 4.3 copy-start.32
  755.1 3.6 copy-start.12
  757.5 163.8 %copy-start.7 = (f32[256,1408]{1,0:T(8,128)}, f32[256,1408]{1,0:T(8,128)S(1)}, u32[]{:S(2)}) copy-start(f32[256,1408]{1,0:T(8,128)S(1)} %fusion.8) | copy-start | bytes 4325380
  760.3 160.1 %reduce-scatter.14.cloned.1.call-start = ((), (), s32[]{:S(2)}) async-start(), calls=%async_computation.12 | async-start | bytes 765952
  847.9 126.8 %copy-start.38 = (s32[1024]{0:T(1024)S(1)}, s32[1024]{0:T(1024)}, u32[]{:S(2)}) copy-start(s32[1024]{0:T(1024)} %copy-done.37) | copy-start | bytes 12292
  847.9 128.2 %copy-start.52 = (pred[512]{0:T(512)(128)(4,1)S(1)}, pred[512]{0:T(512)(128)(4,1)}, u32[]{:S(2)}) copy-start(pred[512]{0:T(512)(128)(4,1)} %copy-done.51) | copy-start | bytes 1540
  847.9 128.2 %copy-start.54 = (pred[512]{0:T(512)(128)(4,1)S(1)}, pred[512]{0:T(512)(128)(4,1)}, u32[]{:S(2)}) copy-start(pred[512]{0:T(512)(128)(4,1)} %copy-done.53) | copy-start | bytes 1540
  847.9 154.2 %copy-start.20 = (f32[49,88]{1,0:T(8,128)S(1)}, f32[49,88]{1,0:T(8,128)}, u32[]{:S(2)}) copy-start(f32[49,88]{1,0:T(8,128)} %param.31) | copy-start | bytes 51748
  847.9 154.2 %copy-start.22 = (f32[49,88]{1,0:T(8,128)S(1)}, f32[49,88]{1,0:T(8,128)}, u32[]{:S(2)}) copy-start(f32[49,88]{1,0:T(8,128)} %copy-done.21) | copy-start | bytes 51748
  (5 other events, 3.3 us)
Sparse Core Ops, SparseCore 0:
  224.8 85.8 all-reduce.13
  315.0 72.4 reduce-scatter.11
  390.7 72.2 reduce-scatter.9
  760.4 83.5 all-reduce.11
  848.1 72.2 reduce-scatter.13
where the time goes:
time: 1100 us; the launch traced here: 1090 us
  waiting for transfers between devices  421 us (38%)
  blocking collectives  388 us (35%)
  other arithmetic  169 us (15%)
  local copies, waits for them, and re-layouts  59.9 us (5%)
  starting transfers between devices  17.3 us (2%)
  between operations  17.1 us (2%)
  matrix products  17 us (2%)
    unnamed x8, waiting for transfers between devices  215 us
    psum x5, blocking collectives, inner_model(): return lax.psum(jnp.sum(first_vec * second_vec), 'mp')  191 us
    psum x2, waiting for transfers between devices, model_sum(): lax.psum(partial_value.astype(jnp.bfloat16), 'mp').astype(jnp.float32)  170 us
    convert_element_type x2, other arithmetic, hessian(): depthwise(conv_source, full_direction).astype(jnp.bfloat16)  100 us
    psum x2, blocking collectives, row_stats(): return lax.psum((first_sum, second_sum), 'mp')  76.2 us
    psum x2, blocking collectives, hessian(): return (lax.psum(local_term, 'dp'), local_term)  47.7 us
    all_gather x2, blocking collectives, hessian(): full_direction = lax.all_gather(direction, 'mp', axis=1, tiled=True)  42.2 us
    all_to_all x1, waiting for transfers between devices, per_device(): lax.all_to_all(pack_slots(payload), 'dp', split_axis=0, concat_axis=0, ti...  24.6 us
  transfers between devices with their start and end apart: 9, of which 8 were waited for; matrix products, arithmetic and copies ran while one was open for 9% of the time, Pallas kernels for 0%

commit v1 on v0

v1 whole, which is shorter than its diff:
```python
import jax
import jax.numpy as jnp
from jax import lax
from jax.experimental import pallas as pl
from jax.experimental.pallas import tpu as pltpu
from jax.sharding import PartitionSpec as P

C = 1408
H = 5632
KS = 7
SIDE = 16
TAPS = 49
TOKENS = 2048
N_MP = 16
N_DP = 8
HPART = H // N_MP
HALF = HPART // 2
QUARTER = HALF // 2
CPART = C // N_MP
ROWS = 32
LANE = 128
CBLK = C // LANE
HBLK = 512
NHB = H // HBLK
TAPROWS = 56
TILES = 80
CHUNK = TILES // N_MP

layer_eps = 1e-06
vector_eps = 1e-06
half_root = 0.7071067811865476
density_scale = 0.3989422804014327

MESH = pl.DeviceIdType.MESH
VMEM_BIG = 64 * 1024 * 1024 - 512 * 1024
F32 = jnp.float32
BF16 = jnp.bfloat16


def vmem():
    return pl.BlockSpec(memory_space=pltpu.VMEM)


def hbm():
    return pl.BlockSpec(memory_space=pl.ANY)


def gather_kernel(
    w1_ref, w2_ref, misc_ref, o1_ref, o2_ref, om_ref, send, recv, fsend, frecv, msend, mrecv, lsem
):
    dp = lax.axis_index("dp")
    mp = lax.axis_index("mp")
    core = lax.rem(dp, 2)
    sib = dp + 1 - 2 * core
    z = mp // 4
    y = lax.rem(mp, 4)

    def at(dz, dy):
        return lax.rem(z + dz, 4) * 4 + lax.rem(y + dy, 4)

    barrier = pltpu.get_barrier_semaphore()
    for r in range(1, N_MP):
        pl.semaphore_signal(
            barrier, inc=1, device_id={"mp": lax.rem(mp + r, N_MP)}, device_id_type=MESH
        )
    pl.semaphore_signal(barrier, inc=1, device_id={"dp": sib}, device_id_type=MESH)
    pl.semaphore_wait(barrier, N_MP)

    base = pl.multiple_of(core * HALF, 8)
    own = (w1_ref, w2_ref)
    out = (o1_ref, o2_ref)
    pending = []

    def remote(src, dst, ssem, rsem, **dev):
        copy = pltpu.make_async_remote_copy(
            src_ref=src, dst_ref=dst, send_sem=ssem, recv_sem=rsem, device_id=dev, device_id_type=MESH
        )
        return copy

    def step(colour, first, second):
        return (second, first) if colour == 0 else (first, second)

    def peer(colour, axis, sign):
        d = 1 if sign == 0 else 3
        a, b = (d, 0) if axis == 0 else (0, d)
        return at(*step(colour, a, b))

    def block(colour, a, b):
        return at(*step(colour, b, a))

    def rows(part):
        if part == 2:
            return pl.ds(base, HALF)
        return pl.ds(pl.multiple_of(base + part * QUARTER, 8), QUARTER)

    slot = {}

    def transfer(colour, key, a, b, part, axis, sign):
        k = slot.setdefault(key, len(slot))
        if (a, b) == (0, 0):
            src = own[colour].at[rows(part)]
        else:
            src = out[colour].at[block(colour, a, b), rows(part)]
        dst = out[colour].at[block(colour, a, b), rows(part)]
        return remote(
            src, dst, send.at[colour, k], recv.at[colour, k], mp=peer(colour, axis, sign)
        )

    started = []

    def go(colour, key, a, b, part, axis, sign):
        copy = transfer(colour, key, a, b, part, axis, sign)
        copy.start()
        started.append(copy)
        pending.append((colour, key))
        return copy

    nforward = [0]
    forwards = []

    def forward(colour, a, b):
        k = nforward[0]
        nforward[0] += 1
        ref = out[colour].at[block(colour, a, b), rows(2)]
        copy = remote(ref, ref, fsend.at[k], frecv.at[k], dp=sib)
        copy.start()
        forwards.append(copy)

    copies = {}
    for colour in range(2):
        for sign in range(2):
            copies[colour, 0, "n", sign] = go(colour, ("n", sign), 0, 0, 2, 0, sign)
    for r in range(1, N_MP):
        copy = remote(
            misc_ref,
            om_ref.at[mp],
            msend.at[r],
            mrecv.at[r],
            mp=lax.rem(mp + r, N_MP),
        )
        copy.start()
        copies["misc", r] = copy
    local = []
    for colour in range(2):
        copy = pltpu.make_async_copy(own[colour], out[colour].at[mp], lsem.at[colour])
        copy.start()
        local.append(copy)
    copy = pltpu.make_async_copy(misc_ref, om_ref.at[mp], lsem.at[2])
    copy.start()
    local.append(copy)

    def spread(colour, b):
        for sign in range(2):
            copies[colour, 1, b, sign] = go(colour, ("z", b, sign), 0, b, 2, 1, sign)

    for colour in range(2):
        spread(colour, 0)
    for sign in range(2):
        for colour in range(2):
            copies[colour, 0, "n", sign].wait_recv()
            b = 3 if sign == 0 else 1
            copies[colour, 0, "r", sign] = go(colour, ("r", sign), 0, b, sign, 0, sign)
            spread(colour, b)
            forward(colour, 0, b)
    for colour in range(2):
        copies[colour, 0, "r", 0].wait_recv()
        copies[colour, 0, "r", 1].wait_recv()
        spread(colour, 2)
        forward(colour, 0, 2)
    for b in (0, 3, 1, 2):
        for sign in range(2):
            for colour in range(2):
                copies[colour, 1, b, sign].wait_recv()
                a = 3 if sign == 0 else 1
                copies[colour, 1, b, "r", sign] = go(
                    colour, ("zr", b, sign), a, b, sign, 1, sign
                )
                forward(colour, a, b)
    for b in (0, 3, 1, 2):
        for colour in range(2):
            copies[colour, 1, b, "r", 0].wait_recv()
            copies[colour, 1, b, "r", 1].wait_recv()
            forward(colour, 2, b)
    for r in range(1, N_MP):
        copies["misc", r].wait_recv()
        copies["misc", r].wait_send()
    for copy in forwards:
        copy.wait_recv()
    for copy in started + forwards:
        copy.wait_send()
    for copy in local:
        copy.wait()


def gather(w1, w2, misc):
    return pl.pallas_call(
        gather_kernel,
        out_shape=(
            jax.ShapeDtypeStruct((N_MP, HPART, C), BF16),
            jax.ShapeDtypeStruct((N_MP, HPART, C), BF16),
            jax.ShapeDtypeStruct((N_MP, 64, LANE), F32),
        ),
        in_specs=[vmem(), vmem(), vmem()],
        out_specs=(hbm(), hbm(), hbm()),
        scratch_shapes=[
            pltpu.SemaphoreType.DMA((2, 20)),
            pltpu.SemaphoreType.DMA((2, 20)),
            pltpu.SemaphoreType.DMA((30,)),
            pltpu.SemaphoreType.DMA((30,)),
            pltpu.SemaphoreType.DMA((N_MP,)),
            pltpu.SemaphoreType.DMA((N_MP,)),
            pltpu.SemaphoreType.DMA((3,)),
        ],
        compiler_params=pltpu.CompilerParams(collective_id=0, has_side_effects=True),
        name="gather_weights",
    )(w1, w2, misc)


def reduce_kernel(p_ref, o_ref, in1, in2, s1, r1, s2, r2, s3, r3):
    dp = lax.axis_index("dp")
    mp = lax.axis_index("mp")
    barrier = pltpu.get_barrier_semaphore()
    for r in range(1, N_MP):
        pl.semaphore_signal(
            barrier, inc=1, device_id={"mp": lax.rem(mp + r, N_MP)}, device_id_type=MESH
        )
    for r in range(1, N_DP):
        pl.semaphore_signal(
            barrier, inc=1, device_id={"dp": lax.rem(dp + r, N_DP)}, device_id_type=MESH
        )
    pl.semaphore_wait(barrier, N_MP + N_DP - 2)

    def send(src, dst, ssem, rsem, **dev):
        copy = pltpu.make_async_remote_copy(
            src_ref=src, dst_ref=dst, send_sem=ssem, recv_sem=rsem, device_id=dev, device_id_type=MESH
        )
        copy.start()
        return copy

    first = []
    for r in range(1, N_MP):
        peer = lax.rem(mp + r, N_MP)
        first.append(
            send(p_ref.at[pl.ds(peer * CHUNK, CHUNK)], in1.at[r], s1.at[r], r1.at[r], mp=peer)
        )
    total = p_ref[pl.ds(mp * CHUNK, CHUNK)]
    for r in range(1, N_MP):
        first[r - 1].wait_recv()
        total = total + in1[r]
    in2[dp] = total
    second = []
    for r in range(1, N_DP):
        peer = lax.rem(dp + r, N_DP)
        second.append(send(in2.at[dp], in2.at[dp], s2.at[r], r2.at[r], dp=peer))
    for copy in second:
        copy.wait_recv()
    total = in2[0]
    for d in range(1, N_DP):
        total = total + in2[d]
    mine = pl.ds(mp * CHUNK, CHUNK)
    o_ref[mine] = total
    third = []
    for r in range(1, N_MP):
        peer = lax.rem(mp + r, N_MP)
        third.append(send(o_ref.at[mine], o_ref.at[mine], s3.at[r], r3.at[r], mp=peer))
    for copy in third:
        copy.wait_recv()
    for copy in first + second + third:
        copy.wait_send()


def all_reduce(part, which):
    return pl.pallas_call(
        reduce_kernel,
        out_shape=jax.ShapeDtypeStruct((TILES, 8, LANE), F32),
        in_specs=[vmem()],
        out_specs=vmem(),
        scratch_shapes=[
            pltpu.VMEM((N_MP, CHUNK, 8, LANE), F32),
            pltpu.VMEM((N_DP, CHUNK, 8, LANE), F32),
            pltpu.SemaphoreType.DMA((N_MP,)),
            pltpu.SemaphoreType.DMA((N_MP,)),
            pltpu.SemaphoreType.DMA((N_DP,)),
            pltpu.SemaphoreType.DMA((N_DP,)),
            pltpu.SemaphoreType.DMA((N_MP,)),
            pltpu.SemaphoreType.DMA((N_MP,)),
        ],
        compiler_params=pltpu.CompilerParams(collective_id=1 + which, has_side_effects=True),
        name="reduce_product",
    )(part)


def rows_dot_t(left, right):
    return lax.dot_general(
        left, right, (((1,), (1,)), ((), ())), preferred_element_type=F32
    )


def rows_dot(left, right):
    return jnp.dot(left, right, preferred_element_type=F32)


def convolve(xf_ref, taps_ref, out_ref, bias_ref=None):
    def body(cb, carry):
        lanes = pl.ds(pl.multiple_of(cb * LANE, LANE), LANE)
        sums = [jnp.zeros((SIDE, LANE), F32) for _ in range(2)]
        for j in range(KS):
            for r in range(KS + 1):
                x = xf_ref[r, pl.ds(j, SIDE), lanes]
                for p in range(2):
                    i = r - p
                    if 0 <= i < KS:
                        sums[p] = sums[p] + x * taps_ref[pl.ds(i * KS + j, 1), lanes]
        for p in range(2):
            value = sums[p]
            if bias_ref is not None:
                value = value + bias_ref[:, lanes]
            out_ref[pl.ds(p * SIDE, SIDE), lanes] = value
        return carry

    lax.fori_loop(0, CBLK, body, 0)


def correlate(xf_ref, grads_ref, out_ref):
    out_ref[...] = jnp.zeros_like(out_ref)

    def body(cb, carry):
        lanes = pl.ds(pl.multiple_of(cb * LANE, LANE), LANE)
        g = [[grads_ref[pl.ds(p * SIDE + 8 * h, 8), lanes] for h in range(2)] for p in range(2)]
        for j in range(KS):
            xs = [
                [xf_ref[r, pl.ds(j + 8 * h, 8), lanes] for h in range(2)] for r in range(KS + 1)
            ]
            for i in range(KS):
                acc = xs[i][0] * g[0][0] + xs[i][1] * g[0][1]
                acc = acc + xs[i + 1][0] * g[1][0] + xs[i + 1][1] * g[1][1]
                tap = i * KS + j
                out_ref[(tap // 8) * CBLK + cb, pl.ds(tap % 8, 1), :] = jnp.sum(
                    acc, axis=0, keepdims=True
                ) * (1.0 / TOKENS)
        return carry

    lax.fori_loop(0, CBLK, body, 0)


def weight_copies(w_hbm, w_vmem, sem):
    return [
        pltpu.make_async_copy(
            w_hbm.at[pl.ds(b * HBLK, HBLK)], w_vmem.at[pl.ds(b * HBLK, HBLK)], sem.at[b]
        )
        for b in range(NHB)
    ]


def wait_block(w_hbm, w_vmem, sem, b):
    part = pl.ds(pl.multiple_of(b * HBLK, HBLK), HBLK)
    pltpu.make_async_copy(w_hbm.at[part], w_vmem.at[part], sem.at[b]).wait()


def hidden(b):
    return pl.ds(pl.multiple_of(b * HBLK, HBLK), HBLK)


def mean_rows(values):
    return jnp.sum(values, axis=1, keepdims=True) * (1.0 / C)


def hessian_rows(
    tan_ref,
    first_pass_ready,
    w1s,
    w2s,
    slope_ref,
    curv_ref,
    tpre_ref,
    acc_ref,
    grads_ref,
    normed,
    dev,
    gain,
    grad_scaled,
    grad_corr,
    back_conv,
    mask,
):
    t = tan_ref[...].astype(BF16).astype(F32)
    lift = mean_rows(normed * t)
    tan_hat = (t - mean_rows(t) - normed * lift) / dev
    rate = lift / dev
    feat = (tan_hat * gain).astype(BF16)
    acc_ref[...] = jnp.zeros_like(acc_ref)

    def forward(b, carry):
        first_pass_ready(b)
        hid = hidden(b)
        tan_pre = rows_dot_t(feat, w1s[hid, :])
        tpre_ref[:, hid] = tan_pre
        act = (slope_ref[:, hid] * tan_pre).astype(BF16)
        acc_ref[...] += rows_dot(act, w2s[hid, :])
        return carry

    lax.fori_loop(0, NHB, forward, 0)
    tan_out = acc_ref[...].astype(BF16)
    acc_ref[...] = jnp.zeros_like(acc_ref)

    def backward(b, carry):
        hid = hidden(b)
        back = rows_dot_t(tan_out, w2s[hid, :])
        back_pre = (back * slope_ref[:, hid] + curv_ref[:, hid] * tpre_ref[:, hid]).astype(BF16)
        acc_ref[...] += rows_dot(back_pre, w1s[hid, :])
        return carry

    lax.fori_loop(0, NHB, backward, 0)
    scaled = acc_ref[...] * gain
    h1 = mean_rows(scaled)
    h2 = mean_rows(scaled * normed + grad_scaled * tan_hat)
    back = (scaled - h1 - tan_hat * grad_corr - normed * h2) / dev - back_conv * rate
    grads_ref[...] = back.astype(BF16).astype(F32) * mask


def first_kernel(
    x_ref,
    diff_ref,
    mask_ref,
    kernel_ref,
    kbias_ref,
    gain_ref,
    nbias_ref,
    ibias_ref,
    obias_ref,
    probe_ref,
    w1_hbm,
    w2_hbm,
    part_ref,
    q_ref,
    slope_ref,
    curv_ref,
    normed_ref,
    dev_ref,
    gs_ref,
    gc_ref,
    bc_ref,
    w1s,
    w2s,
    xf_ref,
    tan_ref,
    acc_ref,
    tpre_ref,
    sem1,
    sem2,
):
    c1 = weight_copies(w1_hbm, w1s, sem1)
    c2 = weight_copies(w2_hbm, w2s, sem2)
    for b in range(NHB):
        c1[b].start()
        c2[b].start()
    xf_ref[...] = x_ref[...].astype(F32)
    probe = probe_ref[...]
    norm = jnp.sqrt(
        jnp.sum(jnp.sum(probe * probe, axis=1, keepdims=True), axis=0, keepdims=True) + vector_eps
    )
    q_ref[...] = probe / norm
    convolve(xf_ref, kernel_ref, tan_ref, kbias_ref)
    values = tan_ref[...].astype(BF16).astype(F32)
    centered = values - mean_rows(values)
    dev = jnp.sqrt(mean_rows(centered * centered) + layer_eps)
    normed = centered / dev
    gain = gain_ref[...]
    feat = (normed * gain + nbias_ref[...]).astype(BF16)
    convolve(xf_ref, q_ref, tan_ref)
    normed_ref[...] = normed
    dev_ref[...] = jnp.broadcast_to(dev, (ROWS, LANE))
    acc_ref[...] = jnp.zeros_like(acc_ref)

    def forward(b, carry):
        hid = hidden(b)
        wait_block(w1_hbm, w1s, sem1, b)
        pre = rows_dot_t(feat, w1s[hid, :]) + ibias_ref[:, hid]
        phi = 0.5 * (1.0 + lax.erf(pre * half_root))
        density = density_scale * jnp.exp(-0.5 * pre * pre)
        slope_ref[:, hid] = phi + pre * density
        curv_ref[:, hid] = density * (2.0 - pre * pre)
        act = (pre * phi).astype(BF16)
        wait_block(w2_hbm, w2s, sem2, b)
        acc_ref[...] += rows_dot(act, w2s[hid, :])
        return carry

    lax.fori_loop(0, NHB, forward, 0)
    residue = (acc_ref[...] + obias_ref[...] - diff_ref[...].astype(F32)).astype(BF16)
    acc_ref[...] = jnp.zeros_like(acc_ref)

    def backward(b, carry):
        hid = hidden(b)
        back = rows_dot_t(residue, w2s[hid, :])
        curv_ref[:, hid] = back * curv_ref[:, hid]
        back_pre = (back * slope_ref[:, hid]).astype(BF16)
        acc_ref[...] += rows_dot(back_pre, w1s[hid, :])
        return carry

    lax.fori_loop(0, NHB, backward, 0)
    grad_scaled = acc_ref[...] * gain
    grad_mean = mean_rows(grad_scaled)
    grad_corr = mean_rows(grad_scaled * normed)
    back_conv = (grad_scaled - grad_mean - normed * grad_corr) / dev
    gs_ref[...] = grad_scaled
    gc_ref[...] = jnp.broadcast_to(grad_corr, (ROWS, LANE))
    bc_ref[...] = back_conv
    hessian_rows(
        tan_ref,
        lambda b: None,
        w1s,
        w2s,
        slope_ref,
        curv_ref,
        tpre_ref,
        acc_ref,
        tan_ref,
        normed,
        dev,
        gain,
        grad_scaled,
        grad_corr,
        back_conv,
        mask_ref[:, 0:1],
    )
    correlate(xf_ref, tan_ref, part_ref)


def first_stage(x, diff, mask, kernel, kbias, gain, nbias, ibias, obias, probe, w1, w2):
    rows_c = jax.ShapeDtypeStruct((ROWS, C), F32)
    rows_h = jax.ShapeDtypeStruct((ROWS, H), F32)
    rows_l = jax.ShapeDtypeStruct((ROWS, LANE), F32)
    return pl.pallas_call(
        first_kernel,
        out_shape=(
            jax.ShapeDtypeStruct((TILES, 8, LANE), F32),
            jax.ShapeDtypeStruct((TAPROWS, C), F32),
            rows_h,
            rows_h,
            rows_c,
            rows_l,
            rows_c,
            rows_l,
            rows_c,
        ),
        in_specs=[vmem()] * 10 + [hbm(), hbm()],
        out_specs=tuple([vmem()] * 9),
        scratch_shapes=[
            pltpu.VMEM((H, C), BF16),
            pltpu.VMEM((H, C), BF16),
            pltpu.VMEM((KS + 1, 24, C), F32),
            pltpu.VMEM((ROWS, C), F32),
            pltpu.VMEM((ROWS, C), F32),
            pltpu.VMEM((ROWS, H), F32),
            pltpu.SemaphoreType.DMA((NHB,)),
            pltpu.SemaphoreType.DMA((NHB,)),
        ],
        compiler_params=pltpu.CompilerParams(vmem_limit_bytes=VMEM_BIG),
        name="first_stage",
    )(x, diff, mask, kernel, kbias, gain, nbias, ibias, obias, probe, w1, w2)


def total(values):
    return jnp.sum(jnp.sum(values, axis=1, keepdims=True), axis=0, keepdims=True)


def untile(w_ref, flat_ref):
    for rb in range(TAPROWS // 8):
        for cb in range(CBLK):
            flat_ref[pl.ds(8 * rb, 8), pl.ds(LANE * cb, LANE)] = w_ref[rb * CBLK + cb]


def second_kernel(
    w_ref,
    x_ref,
    mask_ref,
    gain_ref,
    q_ref,
    slope_ref,
    curv_ref,
    normed_ref,
    dev_ref,
    gs_ref,
    gc_ref,
    bc_ref,
    w1_hbm,
    w2_hbm,
    part_ref,
    q2_ref,
    terms_ref,
    w1s,
    w2s,
    xf_ref,
    tan_ref,
    acc_ref,
    tpre_ref,
    sem1,
    sem2,
):
    c1 = weight_copies(w1_hbm, w1s, sem1)
    c2 = weight_copies(w2_hbm, w2s, sem2)
    for b in range(NHB):
        c1[b].start()
        c2[b].start()
    xf_ref[...] = x_ref[...].astype(F32)
    untile(w_ref, q2_ref)
    product = q2_ref[...]
    q = q_ref[...]
    alpha = total(product * q)
    remainder = product - alpha * q
    beta = jnp.sqrt(total(remainder * remainder) + vector_eps)
    q2_ref[...] = remainder / beta
    terms_ref[pl.ds(0, 8), :] = jnp.broadcast_to(alpha, (8, LANE))
    terms_ref[pl.ds(8, 8), :] = jnp.broadcast_to(beta, (8, LANE))
    convolve(xf_ref, q2_ref, tan_ref)

    def ready(b):
        wait_block(w1_hbm, w1s, sem1, b)
        wait_block(w2_hbm, w2s, sem2, b)

    hessian_rows(
        tan_ref,
        ready,
        w1s,
        w2s,
        slope_ref,
        curv_ref,
        tpre_ref,
        acc_ref,
        tan_ref,
        normed_ref[...],
        dev_ref[:, 0:1],
        gain_ref[...],
        gs_ref[...],
        gc_ref[:, 0:1],
        bc_ref[...],
        mask_ref[:, 0:1],
    )
    correlate(xf_ref, tan_ref, part_ref)


def second_stage(w, x, mask, gain, q, saved, w1, w2):
    return pl.pallas_call(
        second_kernel,
        out_shape=(
            jax.ShapeDtypeStruct((TILES, 8, LANE), F32),
            jax.ShapeDtypeStruct((TAPROWS, C), F32),
            jax.ShapeDtypeStruct((16, LANE), F32),
        ),
        in_specs=[vmem()] * 12 + [hbm(), hbm()],
        out_specs=(vmem(), vmem(), vmem()),
        scratch_shapes=[
            pltpu.VMEM((H, C), BF16),
            pltpu.VMEM((H, C), BF16),
            pltpu.VMEM((KS + 1, 24, C), F32),
            pltpu.VMEM((ROWS, C), F32),
            pltpu.VMEM((ROWS, C), F32),
            pltpu.VMEM((ROWS, H), F32),
            pltpu.SemaphoreType.DMA((NHB,)),
            pltpu.SemaphoreType.DMA((NHB,)),
        ],
        compiler_params=pltpu.CompilerParams(vmem_limit_bytes=VMEM_BIG),
        name="second_stage",
    )(w, x, mask, gain, q, *saved, w1, w2)


def last_kernel(w_ref, q1_ref, q2_ref, terms_ref, out_ref, scal_ref):
    untile(w_ref, out_ref)
    product = out_ref[...]
    q2 = q2_ref[...]
    alpha = total(product * q2)
    beta_one = terms_ref[pl.ds(8, 1), 0:1]
    remainder = product - alpha * q2 - beta_one * q1_ref[...]
    beta = jnp.sqrt(total(remainder * remainder) + vector_eps)
    out_ref[...] = remainder / beta
    lane = lax.broadcasted_iota(jnp.int32, (8, LANE), 1)
    alpha_one = terms_ref[pl.ds(0, 1), 0:1]
    scal_ref[...] = jnp.where(
        lane == 0,
        alpha,
        jnp.where(lane == 1, beta_one, jnp.where(lane == 2, beta, alpha_one)),
    )


def last_stage(w, q1, q2, terms):
    return pl.pallas_call(
        last_kernel,
        out_shape=(
            jax.ShapeDtypeStruct((TAPROWS, C), F32),
            jax.ShapeDtypeStruct((8, LANE), F32),
        ),
        in_specs=[vmem()] * 4,
        out_specs=(vmem(), vmem()),
        name="last_stage",
    )(w, q1, q2, terms)


def per_device(
    canvas,
    target,
    kernel,
    kernel_bias,
    norm_gain,
    norm_bias,
    in_weight,
    in_bias,
    out_weight,
    out_bias,
    probe_vector,
    shapes,
    send_slots,
):
    mp = lax.axis_index("mp")
    misc = jnp.concatenate(
        [
            jnp.pad(probe_vector, ((0, TAPROWS - TAPS), (0, LANE - CPART))),
            jnp.pad(in_bias, (0, 8 * LANE - HPART)).reshape(8, LANE),
        ],
        0,
    )
    w1, w2, misc_all = gather(in_weight, out_weight, misc)
    w1 = w1.reshape(H, C)
    w2 = w2.reshape(H, C)
    probe = misc_all[:, :TAPROWS, :CPART].transpose(1, 0, 2).reshape(TAPROWS, C)
    ibias = misc_all[:, TAPROWS:, :].reshape(N_MP, 8 * LANE)[:, :HPART].reshape(1, H)

    image = mp // 8
    top = 2 * lax.rem(mp, 8)
    side = lax.dynamic_slice_in_dim(shapes, image, 1, 0)[0]
    cells = jnp.arange(SIDE, dtype=jnp.int32)
    picture = lax.dynamic_slice_in_dim(canvas, image, 1, 0)[0]
    inside = ((cells[:, None] < side[0]) & (cells[None, :] < side[1])).astype(BF16)
    masked = jnp.pad(picture * inside[:, :, None], ((3, 3), (3, 5), (0, 0)))
    window = lax.dynamic_slice_in_dim(masked, top, KS + 1, 0)
    mine = lax.dynamic_slice_in_dim(picture, top, 2, 0)
    aim = lax.dynamic_slice(target, (image, top, 0, 0), (1, 2, SIDE, C))[0]
    diff = (aim.astype(F32) - mine.astype(F32)).astype(BF16).reshape(ROWS, C)
    mask = lax.dynamic_slice_in_dim(inside, top, 2, 0).astype(F32).reshape(ROWS, 1)
    mask = jnp.broadcast_to(mask, (ROWS, LANE))

    part, q1, *saved = first_stage(
        window,
        diff,
        mask,
        kernel,
        kernel_bias.reshape(1, C),
        norm_gain.reshape(1, C),
        norm_bias.reshape(1, C),
        ibias,
        out_bias.reshape(1, C),
        probe,
        w1,
        w2,
    )
    product = all_reduce(part, 0)
    part, q2, terms = second_stage(
        product, window, mask, norm_gain.reshape(1, C), q1, saved, w1, w2
    )
    product = all_reduce(part, 1)
    vector, scalars = last_stage(product, q1, q2, terms)
    krylov = lax.dynamic_slice(vector, (0, mp * CPART), (TAPS, CPART))
    return krylov, scalars[0, 3:4], scalars[0, 0:3]


def solution(mesh):
    placed = (
        P("dp", None, None, None),
        P("dp", None, None, None),
        P(),
        P(),
        P(),
        P(),
        P("mp", None),
        P("mp"),
        P("mp", None),
        P(),
        P(None, "mp"),
        P("dp", None),
        P("dp", None, None),
    )
    return jax.shard_map(
        per_device, mesh=mesh, in_specs=placed, out_specs=(P(None, "mp"), P(), P()), check_vma=False
    )
```

time: 1100 us -> 247 us (0.22)
  waiting for transfers between devices: 421 us -> 0 us
  blocking collectives: 388 us -> 0 us
  Pallas kernels: 0 us -> 223 us
  other arithmetic: 169 us -> 5.57 us
  local copies, waits for them, and re-layouts: 59.9 us -> 16.4 us
  starting transfers between devices: 17.3 us -> 0 us
  matrix products: 17 us -> 0 us
  between operations: 17.1 us -> 0.76 us
    psum x9 -> x0, blocking collectives: 315 us -> none  [the longest x5 191 us: inner_model(): return lax.psum(jnp.sum(first_vec * second_vec), 'mp')]
    pallas_call x0 -> x6, Pallas kernels: none -> 223 us  [the longest x1 99.5 us: gather(): pl.pallas_call(gather_kernel, out_shape=(jax.ShapeDtypeStruct((N_MP, HPAR...]
    unnamed x8 -> x0, waiting for transfers between devices: 215 us -> none
    psum x2 -> x0, waiting for transfers between devices: 170 us -> none  [model_sum(): lax.psum(partial_value.astype(jnp.bfloat16), 'mp').astype(jnp.float32)]
    convert_element_type x10 -> x2, other arithmetic: 124 us -> 1.66 us  [the longest x1 1.58 us: per_device(): diff = (aim.astype(F32) - mine.astype(F32)).astype(BF16).reshape(ROWS, C)]
    all_gather x2 -> x0, blocking collectives: 42.2 us -> none  [hessian(): full_direction = lax.all_gather(direction, 'mp', axis=1, tiled=True)]
    all_to_all x4 -> x0, waiting for transfers between devices: 36.5 us -> none  [the longest x1 24.6 us: per_device(): lax.all_to_all(pack_slots(payload), 'dp', split_axis=0, concat_axis=0, ti...]
    gather x12 -> x0, local copies, waits for them, and re-layouts: 33.1 us -> none  [the longest x3 14.5 us: pack_slots(): jnp.take(values, source_cell, axis=0)]
  transfers between devices with their start and end apart: 9 -> 0, of which waited for: 8 -> 0; matrix products, arithmetic and copies ran while one was open for 9% -> 0% of each run, Pallas kernels for 0% -> 0%
where the time goes in v1:
time: 247 us; the launch traced here: 245 us
  Pallas kernels  223 us (90%)
  local copies, waits for them, and re-layouts  16.4 us (7%)
  other arithmetic  5.57 us (2%)
    pallas_call x1, Pallas kernels, gather(): pl.pallas_call(gather_kernel, out_shape=(jax.ShapeDtypeStruct((N_MP, HPAR...  99.5 us
    pallas_call x1, Pallas kernels, first_stage(): pl.pallas_call(first_kernel, out_shape=(jax.ShapeDtypeStruct((TILES, 8, L...  47.5 us
    pallas_call x2, Pallas kernels, all_reduce(): pl.pallas_call(reduce_kernel, out_shape=jax.ShapeDtypeStruct((TILES, 8, L...  47.4 us
    pallas_call x1, Pallas kernels, second_stage(): pl.pallas_call(second_kernel, out_shape=(jax.ShapeDtypeStruct((TILES, 8,...  26 us

profile of v1, /device:TPU:0, one launch (start us, length us, event | category | flops | bytes accessed | tf_op | source)
XLA Modules:
  0.0 245.3 jit_solution(14224634885944921199)
XLA Ops:
  0.6 0.0 copy-start
  0.7 0.6 copy-done
  1.3 0.6 fusion.1
  1.9 1.3 iota_compare_fusion.1
  3.2 0.1 and_convert_fusion
  3.3 0.1 reshape.99
  3.4 0.7 pad_bitcast_fusion
  4.1 1.3 reshape.90.gain_ref
  5.4 1.3 reshape.89.kbias_ref
  6.7 1.3 reshape.91.nbias_ref
  7.9 1.3 reshape.95.obias_ref
  9.2 0.7 broadcast_in_dim.15.mask_ref
  9.9 1.4 select_maximum_fusion.misc_ref
  11.3 1.6 subtract_convert_fusion
  12.8 1.2 bitcast_multiply_fusion
  14.1 1.0 pad_dynamic-slice_fusion.x_ref
  15.1 99.5 %gather_weights.1 = (bf16[16,352,1408]{2,1,0:T(8,128)(2,1)}, bf16[16,352,1408]{2,1,0:T(8,128)(2,1)}, f32[16,64,128]{2,1,0:T(8,128)}) custom-call(bf16[352,1408]{1,0:T(8,128)(2,1)} %w1_ref.1, bf16[352,1408]{1,0:T(8,128)(2,1)} %w2_ref.1, f32[64,128]{1,0:T(8,128)} %select_maximum_fusion.misc_ref), custom_call_target="tpu_custom_call" | custom-call | tf_op jit(solution)/shard_map/gather_weights/pallas_call | solution.py:196
  114.6 0.8 slice.25
  115.5 1.1 slice_bitcast_fusion
  116.5 0.1 copy.15
  116.6 0.9 reshape.96.probe_ref
  117.6 0.7 reshape.94.ibias_ref
  118.3 47.5 %first_stage.1 = (f32[80,8,128]{2,1,0:T(8,128)}, f32[56,1408]{1,0:T(8,128)}, f32[32,5632]{1,0:T(8,128)}, f32[32,5632]{1,0:T(8,128)}, f32[32,1408]{1,0:T(8,128)},...) custom-call(bf16[8,24,1408]{2,1,0:T(8,128)(2,1)} %pad_dynamic-slice_fusion.x_ref, ...), custom_call_target="tpu_custom_call" | custom-call | tf_op jit(solution)/shard_map/first_stage/pallas_call | solution.py:533
  165.8 25.2 %reduce_product.2.w_ref = f32[80,8,128]{2,1,0:T(8,128)} custom-call(f32[80,8,128]{2,1,0:T(8,128)} %get-tuple-element.23.p_ref), custom_call_target="tpu_custom_call" | custom-call | tf_op jit(solution)/shard_map/reduce_product/pallas_call | solution.py:273
  191.0 26.0 %second_stage.1 = (f32[80,8,128]{2,1,0:T(8,128)}, f32[56,1408]{1,0:T(8,128)}, f32[16,128]{1,0:T(8,128)}) custom-call(f32[80,8,128]{2,1,0:T(8,128)} %reduce_product.2.w_ref, bf16[8,24,1408]{2,1,0:T(8,128)(2,1)} %pad_dynamic-slice_fusion.x_ref, f32[32,128]{1,0:T(8,128)} %broadcast_in_dim.15.mask_ref, f32[1,1408]{1,0:T(1,128)} %reshape.90.gain_ref, ...), custom_call_target="tpu_custom_call" | custom-call | tf_op jit(solution)/shard_map/second_stage/pallas_call | solution.py:643
  216.9 22.2 %reduce_product.3.w_ref = f32[80,8,128]{2,1,0:T(8,128)} custom-call(f32[80,8,128]{2,1,0:T(8,128)} %get-tuple-element.32.p_ref), custom_call_target="tpu_custom_call" | custom-call | tf_op jit(solution)/shard_map/reduce_product/pallas_call | solution.py:273
  239.1 2.2 last_stage.1
  241.3 1.3 slice.28
  242.6 1.5 constant_dynamic-slice_fusion.1
  244.1 1.2 slice_bitcast_fusion.1
  (4 shorter events, 0.0 us)
Async XLA Ops:
  0.6 0.7 copy-start

commit v2 on v0

v2 whole, which is shorter than its diff:
```python
import jax
import jax.numpy as jnp
from jax import lax
from jax.experimental import pallas as pl
from jax.experimental.pallas import tpu as pltpu
from jax.sharding import PartitionSpec as P

C = 1408
H = 5632
KS = 7
SIDE = 16
TAPS = 49
TOKENS = 2048
N_MP = 16
N_DP = 8
HPART = H // N_MP
HALF = HPART // 2
CPART = C // N_MP
ROWS = 32
LANE = 128
CBLK = C // LANE
HBLK = 1408
NHB = H // HBLK
TAPROWS = 56
TILES = 80
CHUNK = TILES // N_MP

EDGE = 64
MIDDLE = HALF - 2 * EDGE
PLANE = EDGE + MIDDLE
LAG_X = 4
LAG_FORWARD = 7

layer_eps = 1e-06
vector_eps = 1e-06
half_root = 0.7071067811865476
density_scale = 0.3989422804014327

MESH = pl.DeviceIdType.MESH
VMEM_BIG = 64 * 1024 * 1024 - 512 * 1024
F32 = jnp.float32
BF16 = jnp.bfloat16


def vmem():
    return pl.BlockSpec(memory_space=pltpu.VMEM)


def hbm():
    return pl.BlockSpec(memory_space=pl.ANY)


def rows_dot_t(left, right):
    return lax.dot_general(
        left, right, (((1,), (1,)), ((), ())), preferred_element_type=F32
    )


def rows_dot(left, right):
    return jnp.dot(left, right, preferred_element_type=F32)


def mean_rows(values):
    return jnp.sum(values, axis=1, keepdims=True) * (1.0 / C)


def total(values):
    return jnp.sum(jnp.sum(values, axis=1, keepdims=True), axis=0, keepdims=True)


def hidden(b):
    return pl.ds(pl.multiple_of(b * HBLK, HBLK), HBLK)


def convolve(xf_ref, taps_ref, out_ref, bias=None):
    def body(cb, carry):
        lanes = pl.ds(pl.multiple_of(cb * LANE, LANE), LANE)
        sums = [jnp.zeros((SIDE, LANE), F32) for _ in range(2)]
        for j in range(KS):
            for r in range(KS + 1):
                x = xf_ref[r, pl.ds(j, SIDE), lanes]
                for p in range(2):
                    i = r - p
                    if 0 <= i < KS:
                        sums[p] = sums[p] + x * taps_ref[pl.ds(i * KS + j, 1), lanes]
        for p in range(2):
            value = sums[p]
            if bias is not None:
                value = value + bias[pl.ds(0, 1), lanes]
            out_ref[pl.ds(p * SIDE, SIDE), lanes] = value
        return carry

    lax.fori_loop(0, CBLK, body, 0)


def correlate(xf_ref, grads_ref, out_ref):
    out_ref[...] = jnp.zeros_like(out_ref)

    def body(cb, carry):
        lanes = pl.ds(pl.multiple_of(cb * LANE, LANE), LANE)
        g = [[grads_ref[pl.ds(p * SIDE + 8 * h, 8), lanes] for h in range(2)] for p in range(2)]
        for j in range(KS):
            xs = [
                [xf_ref[r, pl.ds(j + 8 * h, 8), lanes] for h in range(2)] for r in range(KS + 1)
            ]
            for i in range(KS):
                acc = xs[i][0] * g[0][0] + xs[i][1] * g[0][1]
                acc = acc + xs[i + 1][0] * g[1][0] + xs[i + 1][1] * g[1][1]
                tap = i * KS + j
                out_ref[(tap // 8) * CBLK + cb, pl.ds(tap % 8, 1), :] = jnp.sum(
                    acc, axis=0, keepdims=True
                ) * (1.0 / TOKENS)
        return carry

    lax.fori_loop(0, CBLK, body, 0)


def untile(w_ref, flat_ref):
    for rb in range(TAPROWS // 8):
        for cb in range(CBLK):
            flat_ref[pl.ds(8 * rb, 8), pl.ds(LANE * cb, LANE)] = w_ref[rb * CBLK + cb]


def send(src, dst, ssem, rsem, **dev):
    copy = pltpu.make_async_remote_copy(
        src_ref=src, dst_ref=dst, send_sem=ssem, recv_sem=rsem, device_id=dev, device_id_type=MESH
    )
    copy.start()
    return copy


def all_reduce(p_ref, o_ref, in1, in2, sems):
    dp = lax.axis_index("dp")
    mp = lax.axis_index("mp")
    s1, r1, s2, r2, s3, r3 = sems
    first = []
    for r in range(1, N_MP):
        peer = lax.rem(mp + r, N_MP)
        first.append(
            send(p_ref.at[pl.ds(peer * CHUNK, CHUNK)], in1.at[r], s1.at[r], r1.at[r], mp=peer)
        )
    value = p_ref[pl.ds(mp * CHUNK, CHUNK)]
    for r in range(1, N_MP):
        first[r - 1].wait_recv()
        value = value + in1[r]
    in2[dp] = value
    second = []
    for r in range(1, N_DP):
        peer = lax.rem(dp + r, N_DP)
        second.append(send(in2.at[dp], in2.at[dp], s2.at[r], r2.at[r], dp=peer))
    for copy in second:
        copy.wait_recv()
    value = in2[0]
    for d in range(1, N_DP):
        value = value + in2[d]
    mine = pl.ds(mp * CHUNK, CHUNK)
    o_ref[mine] = value
    third = []
    for r in range(1, N_MP):
        peer = lax.rem(mp + r, N_MP)
        third.append(send(o_ref.at[mine], o_ref.at[mine], s3.at[r], r3.at[r], mp=peer))
    for copy in third:
        copy.wait_recv()
    return first + second + third


def lanczos_kernel(
    w1_ref,
    w2_ref,
    probe_ref,
    bias_ref,
    vec_ref,
    kernel_ref,
    shapes_ref,
    canvas_ref,
    target_ref,
    out_ref,
    scal_ref,
    w1s,
    w2s,
    probes,
    biases,
    xb_ref,
    tb_ref,
    xf_ref,
    tan_ref,
    acc_ref,
    slope_ref,
    curv_ref,
    tpre_ref,
    normed_ref,
    feat_ref,
    q_ref,
    q2_ref,
    part_ref,
    part2_ref,
    prod_ref,
    prod2_ref,
    in1a,
    in2a,
    in1b,
    in2b,
    psend,
    precv,
    xsend,
    xrecv,
    fsend,
    frecv,
    msend,
    mrecv,
    lsem,
    *arsems,
):
    dp = lax.axis_index("dp")
    mp = lax.axis_index("mp")
    core = lax.rem(dp, 2)
    x = dp // 2
    odd = lax.rem(x, 2)
    sib = dp + 1 - 2 * core
    z = mp // 4
    y = lax.rem(mp, 4)

    def at(dz, dy):
        return lax.rem(z + dz, 4) * 4 + lax.rem(y + dy, 4)

    barrier = pltpu.get_barrier_semaphore()
    for r in range(1, N_MP):
        pl.semaphore_signal(
            barrier, inc=1, device_id={"mp": lax.rem(mp + r, N_MP)}, device_id_type=MESH
        )
    for r in range(1, N_DP):
        pl.semaphore_signal(
            barrier, inc=1, device_id={"dp": lax.rem(dp + r, N_DP)}, device_id_type=MESH
        )

    image = mp // 8
    top = 2 * lax.rem(mp, 8)
    local = []

    def fetch(src, dst):
        copy = pltpu.make_async_copy(src, dst, lsem.at[len(local)])
        copy.start()
        local.append(copy)

    for r in range(KS + 1):
        row = lax.rem(top + r + SIDE - 3, SIDE)
        fetch(canvas_ref.at[image, row], xb_ref.at[r])
    for p in range(2):
        fetch(target_ref.at[image, top + p], tb_ref.at[p])
    fetch(w1_ref, w1s.at[pl.ds(0, HPART)])
    fetch(w2_ref, w2s.at[pl.ds(0, HPART)])
    fetch(probe_ref, probes.at[mp])
    fetch(bias_ref, biases.at[0])

    pl.semaphore_wait(barrier, N_MP + N_DP - 2)

    own = (w1_ref, w2_ref)
    ws = (w1s, w2s)
    started = []

    def offsets(colour, first, second):
        return (second, first) if colour == 0 else (first, second)

    def slot_of(dz, dy):
        return (dz % 4) * 4 + dy % 4

    def rows(slot, off, n):
        return pl.ds(pl.multiple_of(slot * HPART + core * HALF + off, 16), n)

    keys = [{}, {}]

    def go(colour, key, first, second, off, n, axis, sign):
        k = keys[colour].setdefault(key, len(keys[colour]))
        dz, dy = offsets(colour, first, second)
        move = 1 if sign == 0 else 3
        pz, py = offsets(colour, *((move, 0) if axis == 0 else (0, move)))
        src = own[colour] if (dz, dy) == (0, 0) else ws[colour]
        copy = send(
            src.at[rows(slot_of(dz, dy), off, n)],
            ws[colour].at[rows(slot_of(dz - pz, dy - py), off, n)],
            psend.at[colour, k],
            precv.at[colour, k],
            mp=at(pz, py),
        )
        started.append(copy)
        return copy

    plane_off = odd * EDGE
    copies = {}

    def relay_cut(flag):
        return PLANE // 2 // 16 * 16 + (16 if flag else 0) if PLANE // 2 % 16 else PLANE // 2

    def relay(colour, key, first, second, axis, sign, flag):
        cut = relay_cut(flag)
        off, n = (0, cut) if sign == 0 else (cut, PLANE - cut)
        copies[colour, key] = go(colour, key, first, second, plane_off + off, n, axis, sign)

    def spread(colour, first):
        for sign in range(2):
            key = ("s", first, sign)
            copies[colour, key] = go(colour, key, first, 0, plane_off, PLANE, 1, sign)

    xcopies = {}
    fcopies = {}

    def share(colour, first, second):
        dz, dy = offsets(colour, first, second)
        slot = slot_of(dz, dy)
        for sign in range(2):
            move = 1 if sign == 0 else 3
            piece = rows(slot, odd * PLANE + sign * (EDGE // 2), EDGE // 2)
            copy = send(
                ws[colour].at[piece],
                ws[colour].at[piece],
                xsend.at[colour, slot, sign],
                xrecv.at[colour, slot, sign],
                dp=lax.rem(x + move, 4) * 2 + core,
            )
            started.append(copy)
            xcopies[colour, slot, sign] = copy

    def forward(colour, slot, kind, off, n):
        piece = rows(slot, off, n)
        copy = send(
            ws[colour].at[piece],
            ws[colour].at[piece],
            fsend.at[colour, slot, kind],
            frecv.at[colour, slot, kind],
            dp=sib,
        )
        started.append(copy)
        fcopies[colour, slot, kind] = copy

    for colour in range(2):
        for sign in range(2):
            key = ("n", sign)
            copies[colour, key] = go(colour, key, 0, 0, plane_off, PLANE, 0, sign)
    for dz in range(4):
        for dy in range(4):
            if dz or dy:
                k = slot_of(dz, dy)
                copy = send(probe_ref, probes.at[mp], msend.at[0, k], mrecv.at[0, k], mp=at(dz, dy))
                started.append(copy)
                copies["probe", k] = copy
                k = slot_of(-dz, -dy)
                copy = send(
                    bias_ref, biases.at[k], msend.at[1, k], mrecv.at[1, k], mp=at(dz, dy)
                )
                started.append(copy)
                copies["bias", k] = copy
    for colour in range(2):
        spread(colour, 0)

    for copy in local:
        copy.wait()
    high = shapes_ref[image, 0]
    wide = shapes_ref[image, 1]
    column = lax.broadcasted_iota(jnp.int32, (SIDE, LANE), 0)
    in_row = jnp.where(column < wide, 1.0, 0.0)[:, 0:1]
    xf_ref[...] = jnp.zeros_like(xf_ref)
    for r in range(KS + 1):
        row = top + r - 3
        valid = jnp.where((row >= 0) & (row < high), 1.0, 0.0)
        xf_ref[r, pl.ds(3, SIDE), :] = xb_ref[r].astype(F32) * (in_row * valid)
    cell = lax.broadcasted_iota(jnp.int32, (ROWS, LANE), 0)
    lower = jnp.where(cell >= SIDE, 1, 0)
    mask = jnp.where((top + lower < high) & (cell - SIDE * lower < wide), 1.0, 0.0)[:, 0:1]
    gain = vec_ref[pl.ds(1, 1), :]

    convolve(xf_ref, kernel_ref, tan_ref, vec_ref)
    values = tan_ref[...].astype(BF16).astype(F32)
    centered = values - mean_rows(values)
    dev = jnp.sqrt(mean_rows(centered * centered) + layer_eps)
    normed = centered / dev
    normed_ref[...] = normed
    feat_ref[...] = (normed * gain + vec_ref[pl.ds(2, 1), :]).astype(BF16)
    acc_ref[...] = jnp.zeros_like(acc_ref)

    def run_block(slot):
        part = pl.ds(slot * HPART, HPART)
        pre = rows_dot_t(feat_ref[...], w1s[part, :]) + biases[slot][:, :HPART]
        phi = 0.5 * (1.0 + lax.erf(pre * half_root))
        density = density_scale * jnp.exp(-0.5 * pre * pre)
        slope_ref[:, part] = phi + pre * density
        curv_ref[:, part] = density * (2.0 - pre * pre)
        act = (pre * phi).astype(BF16)
        acc_ref[...] += rows_dot(act, w2s[part, :])

    events = []
    for sign in range(2):
        for colour in range(2):
            events.append((colour, 3 if sign == 0 else 1, 0, [("n", sign)]))
    for colour in range(2):
        events.append((colour, 2, 0, [("r", 0), ("r", 1)]))
    for first in (0, 3, 1, 2):
        for sign in range(2):
            for colour in range(2):
                events.append((colour, first, 3 if sign == 0 else 1, [("s", first, sign)]))
    for first in (0, 3, 1, 2):
        for colour in range(2):
            events.append((colour, first, 2, [("t", first, 0), ("t", first, 1)]))
    ready = {}
    queue = []

    def finish_x(index):
        colour, first, second, _ = events[index]
        slot = slot_of(*offsets(colour, first, second))
        for sign in range(2):
            xcopies[colour, slot, sign].wait_recv()
        forward(colour, slot, 1, (1 - odd) * PLANE, EDGE)
        ready[slot] = ready.get(slot, 0) + 1
        if ready[slot] == 2:
            queue.append((index, slot))

    def finish_block(slot):
        for colour in range(2):
            for kind in range(2):
                fcopies[colour, slot, kind].wait_recv()
        copies["bias", slot].wait_recv()
        run_block(slot)

    for index, (colour, first, second, waits) in enumerate(events):
        for key in waits:
            copies[colour, key].wait_recv()
        kind = waits[0][0]
        if kind == "n":
            sign = waits[0][1]
            relay(colour, ("r", sign), first, 0, 0, sign, colour)
        if kind in "nr":
            spread(colour, first)
        if kind == "s":
            sign = waits[0][2]
            relay(colour, ("t", first, sign), first, second, 1, sign, first % 2)
        share(colour, first, second)
        slot = slot_of(*offsets(colour, first, second))
        forward(colour, slot, 0, plane_off, PLANE)
        if index == 3:
            run_block(0)
        if index >= LAG_X:
            finish_x(index - LAG_X)
        while queue and queue[0][0] + LAG_FORWARD <= index:
            finish_block(queue.pop(0)[1])
        if index == 8:
            for k in range(1, N_MP):
                copies["probe", k].wait_recv()
            for i in range(N_MP):
                q_ref[:, pl.ds(i * CPART, CPART)] = probes[i][:, :CPART]
            probe = q_ref[...]
            q_ref[...] = probe / jnp.sqrt(total(probe * probe) + vector_eps)
            convolve(xf_ref, q_ref, tan_ref)
    for index in range(len(events) - LAG_X, len(events)):
        finish_x(index)
        if queue:
            finish_block(queue.pop(0)[1])
    while queue:
        finish_block(queue.pop(0)[1])

    diff = jnp.concatenate(
        [
            tb_ref[p].astype(F32) - xb_ref[3 + p].astype(F32)
            for p in range(2)
        ],
        axis=0,
    ).astype(BF16)
    residue = (acc_ref[...] + vec_ref[pl.ds(3, 1), :] - diff.astype(F32)).astype(BF16)
    acc_ref[...] = jnp.zeros_like(acc_ref)

    def backward(b, carry):
        hid = hidden(b)
        back = rows_dot_t(residue, w2s[hid, :])
        curv_ref[:, hid] = back * curv_ref[:, hid]
        back_pre = (back * slope_ref[:, hid]).astype(BF16)
        acc_ref[...] += rows_dot(back_pre, w1s[hid, :])
        return carry

    lax.fori_loop(0, NHB, backward, 0)
    grad_scaled = acc_ref[...] * gain
    normed = normed_ref[...]
    grad_corr = mean_rows(grad_scaled * normed)
    back_conv = (grad_scaled - mean_rows(grad_scaled) - normed * grad_corr) / dev

    def hessian(to_ref):
        t = tan_ref[...].astype(BF16).astype(F32)
        lift = mean_rows(normed * t)
        tan_hat = (t - mean_rows(t) - normed * lift) / dev
        rate = lift / dev
        feat = (tan_hat * gain).astype(BF16)
        acc_ref[...] = jnp.zeros_like(acc_ref)

        def up(b, carry):
            hid = hidden(b)
            tan_pre = rows_dot_t(feat, w1s[hid, :])
            tpre_ref[:, hid] = tan_pre
            act = (slope_ref[:, hid] * tan_pre).astype(BF16)
            acc_ref[...] += rows_dot(act, w2s[hid, :])
            return carry

        lax.fori_loop(0, NHB, up, 0)
        tan_out = acc_ref[...].astype(BF16)
        acc_ref[...] = jnp.zeros_like(acc_ref)

        def down(b, carry):
            hid = hidden(b)
            back = rows_dot_t(tan_out, w2s[hid, :])
            back_pre = (
                back * slope_ref[:, hid] + curv_ref[:, hid] * tpre_ref[:, hid]
            ).astype(BF16)
            acc_ref[...] += rows_dot(back_pre, w1s[hid, :])
            return carry

        lax.fori_loop(0, NHB, down, 0)
        scaled = acc_ref[...] * gain
        h1 = mean_rows(scaled)
        h2 = mean_rows(scaled * normed + grad_scaled * tan_hat)
        back = (scaled - h1 - tan_hat * grad_corr - normed * h2) / dev - back_conv * rate
        tan_ref[...] = back.astype(BF16).astype(F32) * mask
        correlate(xf_ref, tan_ref, to_ref)

    hessian(part_ref)
    reduced = all_reduce(part_ref, prod_ref, in1a, in2a, arsems[:6])
    untile(prod_ref, q2_ref)
    product = q2_ref[...]
    alpha_one = total(product * q_ref[...])
    remainder = product - alpha_one * q_ref[...]
    beta_one = jnp.sqrt(total(remainder * remainder) + vector_eps)
    q2_ref[...] = remainder / beta_one
    convolve(xf_ref, q2_ref, tan_ref)
    hessian(part2_ref)
    reduced = reduced + all_reduce(part2_ref, prod2_ref, in1b, in2b, arsems[6:])
    untile(prod2_ref, out_ref)
    product = out_ref[...]
    alpha_two = total(product * q2_ref[...])
    remainder = product - alpha_two * q2_ref[...] - beta_one * q_ref[...]
    beta_two = jnp.sqrt(total(remainder * remainder) + vector_eps)
    out_ref[...] = remainder / beta_two
    lane = lax.broadcasted_iota(jnp.int32, (8, LANE), 1)
    scal_ref[...] = jnp.where(
        lane == 0,
        alpha_two,
        jnp.where(lane == 1, beta_one, jnp.where(lane == 2, beta_two, alpha_one)),
    )
    for copy in started + reduced:
        copy.wait_send()


def lanczos(*args):
    dma = pltpu.SemaphoreType.DMA
    cells_c = pltpu.VMEM((ROWS, C), F32)
    cells_h = pltpu.VMEM((ROWS, H), F32)
    taps_c = pltpu.VMEM((TAPROWS, C), F32)
    tiles = pltpu.VMEM((TILES, 8, LANE), F32)
    from_mp = pltpu.VMEM((N_MP, CHUNK, 8, LANE), F32)
    from_dp = pltpu.VMEM((N_DP, CHUNK, 8, LANE), F32)
    return pl.pallas_call(
        lanczos_kernel,
        out_shape=(
            jax.ShapeDtypeStruct((TAPROWS, C), F32),
            jax.ShapeDtypeStruct((8, LANE), F32),
        ),
        in_specs=[vmem()] * 6 + [pl.BlockSpec(memory_space=pltpu.SMEM), hbm(), hbm()],
        out_specs=(vmem(), vmem()),
        scratch_shapes=[
            pltpu.VMEM((H, C), BF16),
            pltpu.VMEM((H, C), BF16),
            pltpu.VMEM((N_MP, TAPROWS, LANE), F32),
            pltpu.VMEM((N_MP, 1, 3 * LANE), F32),
            pltpu.VMEM((KS + 1, SIDE, C), BF16),
            pltpu.VMEM((2, SIDE, C), BF16),
            pltpu.VMEM((KS + 1, 24, C), F32),
            cells_c,
            cells_c,
            cells_h,
            cells_h,
            cells_h,
            cells_c,
            pltpu.VMEM((ROWS, C), BF16),
            taps_c,
            taps_c,
            tiles,
            tiles,
            tiles,
            tiles,
            from_mp,
            from_dp,
            from_mp,
            from_dp,
            dma((2, 20)),
            dma((2, 20)),
            dma((2, N_MP, 2)),
            dma((2, N_MP, 2)),
            dma((2, N_MP, 2)),
            dma((2, N_MP, 2)),
            dma((2, N_MP)),
            dma((2, N_MP)),
            dma((KS + 7,)),
        ]
        + 2 * [dma((N_MP,)), dma((N_MP,)), dma((N_DP,)), dma((N_DP,)), dma((N_MP,)), dma((N_MP,))],
        compiler_params=pltpu.CompilerParams(
            collective_id=0, has_side_effects=True, vmem_limit_bytes=VMEM_BIG
        ),
        name="lanczos",
    )(*args)


def per_device(
    canvas,
    target,
    kernel,
    kernel_bias,
    norm_gain,
    norm_bias,
    in_weight,
    in_bias,
    out_weight,
    out_bias,
    probe_vector,
    shapes,
    send_slots,
):
    mp = lax.axis_index("mp")
    vector, scalars = lanczos(
        in_weight,
        out_weight,
        jnp.pad(probe_vector, ((0, TAPROWS - TAPS), (0, LANE - CPART))),
        jnp.pad(in_bias, (0, 3 * LANE - HPART)).reshape(1, 3 * LANE),
        jnp.stack([kernel_bias, norm_gain, norm_bias, out_bias]),
        kernel,
        shapes,
        canvas,
        target,
    )
    krylov = lax.dynamic_slice(vector, (0, mp * CPART), (TAPS, CPART))
    return krylov, scalars[0, 3:4], scalars[0, 0:3]


def solution(mesh):
    placed = (
        P("dp", None, None, None),
        P("dp", None, None, None),
        P(),
        P(),
        P(),
        P(),
        P("mp", None),
        P("mp"),
        P("mp", None),
        P(),
        P(None, "mp"),
        P("dp", None),
        P("dp", None, None),
    )
    return jax.shard_map(
        per_device, mesh=mesh, in_specs=placed, out_specs=(P(None, "mp"), P(), P()), check_vma=False
    )
```

time: 1100 us -> 196 us (0.18)
  waiting for transfers between devices: 421 us -> 0 us
  blocking collectives: 388 us -> 0 us
  Pallas kernels: 0 us -> 184 us
  other arithmetic: 169 us -> 0.63 us
  local copies, waits for them, and re-layouts: 59.9 us -> 9.39 us
  starting transfers between devices: 17.3 us -> 0 us
  matrix products: 17 us -> 0 us
  between operations: 17.1 us -> 0.65 us
    psum x9 -> x0, blocking collectives: 315 us -> none  [the longest x5 191 us: inner_model(): return lax.psum(jnp.sum(first_vec * second_vec), 'mp')]
    unnamed x8 -> x0, waiting for transfers between devices: 215 us -> none
    pallas_call x0 -> x1, Pallas kernels: none -> 184 us  [lanczos(): pl.pallas_call(lanczos_kernel, out_shape=(jax.ShapeDtypeStruct((TAPROWS,...]
    psum x2 -> x0, waiting for transfers between devices: 170 us -> none  [model_sum(): lax.psum(partial_value.astype(jnp.bfloat16), 'mp').astype(jnp.float32)]
    convert_element_type x10 -> x0, other arithmetic: 124 us -> none  [the longest x2 100 us: hessian(): depthwise(conv_source, full_direction).astype(jnp.bfloat16)]
    all_gather x2 -> x0, blocking collectives: 42.2 us -> none  [hessian(): full_direction = lax.all_gather(direction, 'mp', axis=1, tiled=True)]
    all_to_all x4 -> x0, waiting for transfers between devices: 36.5 us -> none  [the longest x1 24.6 us: per_device(): lax.all_to_all(pack_slots(payload), 'dp', split_axis=0, concat_axis=0, ti...]
    gather x12 -> x0, local copies, waits for them, and re-layouts: 33.1 us -> none  [the longest x3 14.5 us: pack_slots(): jnp.take(values, source_cell, axis=0)]
  transfers between devices with their start and end apart: 9 -> 0, of which waited for: 8 -> 0; matrix products, arithmetic and copies ran while one was open for 9% -> 0% of each run, Pallas kernels for 0% -> 0%
where the time goes in v2:
time: 196 us; the launch traced here: 195 us
  Pallas kernels  184 us (94%)
  local copies, waits for them, and re-layouts  9.39 us (5%)
    pallas_call x1, Pallas kernels, lanczos(): pl.pallas_call(lanczos_kernel, out_shape=(jax.ShapeDtypeStruct((TAPROWS,...  184 us

profile of v2, /device:TPU:0, one launch (start us, length us, event | category | flops | bytes accessed | tf_op | source)
XLA Modules:
  0.0 194.6 jit_solution(7736912022289082109)
XLA Ops:
  0.6 1.4 pad.8.probe_ref
  2.0 0.7 pad.9
  2.7 0.6 reshape.9.bias_ref
  3.3 0.7 stack.18
  4.0 0.7 stack.17
  4.7 0.7 stack.16
  5.4 0.7 stack.15
  6.1 0.6 pad_maximum_fusion.vec_ref
  6.7 183.9 %lanczos.1 = (f32[56,1408]{1,0:T(8,128)}, f32[8,128]{1,0:T(8,128)}) custom-call(bf16[352,1408]{1,0:T(8,128)(2,1)} %w1_ref.1, bf16[352,1408]{1,0:T(8,128)(2,1)} %w2_ref.1, f32[56,128]{1,0:T(8,128)} %pad.8.probe_ref, f32[1,384]{1,0:T(1,128)} %reshape.9.bias_ref, f32[4,1408]{1,0:T(4,128)} %pad_maximum_fusion.vec_ref, f32[49,1408]{1,0:T(8,128)} %kernel_ref.1, ...), custom_call_target="tpu_custom_call" | custom-call | tf_op jit(solution)/shard_map/lanczos/pallas_call | solution.py:555
  190.7 1.5 constant_dynamic-slice_fusion
  192.2 1.3 slice.6
  193.4 1.2 slice_bitcast_fusion
